TPU v7x, 32 devices: a whole 2x2x4 slice. The times are simulated.
32 devices in a mesh: coord: 8 (over z, y), cohort: 4 (over x, core).
Axes of the slice: x: 2, y: 2, z: 4, core: 2. Of those that a mesh axis runs over, the one named last changes fastest.
Arguments:
- shapes: bfloat16 [4, 1024, 32768], P('cohort', None, 'coord'), may hold values from -6 to 6
- sketch_signs: int32 [4, 1024, 128], P('cohort'), may hold values from -1 to 1
- merge_sketch: float32 [2, 2, 128, 128], replicated, may hold values from -1.5 to 1.5
Outputs:
- basis: float32 [4, 32768, 128], P('cohort', 'coord')
- scores: float32 [4, 1024, 128], P('cohort', 'coord')
All inputs are finite; a program needn't handle non-finite values.
Results may differ from a plain program's by a relative error of at most 0.0086.
Values sent between devices are 32-bit elements; how exact they have to be, the bound alone decides.
A program may use at most 64 MiB of HBM per device.

v0:
```python
import functools
import math

import jax
import jax.numpy as jnp
from jax import lax
from jax.experimental import pallas as pl
from jax.experimental.pallas import tpu as pltpu
from jax.sharding import PartitionSpec as P

LEVELS = 2
HIGHEST = lax.Precision.HIGHEST
MESH = pl.DeviceIdType.MESH
VMEM = pl.BlockSpec(memory_space=pltpu.VMEM)


def peers_of(n, pair):
    coord = lax.axis_index("coord")
    if not pair:
        return coord, n, lambda rank: {"coord": rank}
    cohort = lax.axis_index("cohort")
    side = lax.rem(cohort, 2)
    base = cohort - side
    rank = coord * 2 + side
    return rank, 2 * n, lambda r: {"coord": r // 2, "cohort": base + lax.rem(r, 2)}


def greet(me, size, ident):
    barrier = pltpu.get_barrier_semaphore()
    for d in range(1, size):
        pl.semaphore_signal(
            barrier, inc=1, device_id=ident(lax.rem(me + d, size)), device_id_type=MESH
        )
    return barrier


def send_block(part_ref, recv, me, size, ident, send, got, d):
    peer = lax.rem(me + d, size)
    return pltpu.make_async_remote_copy(
        src_ref=part_ref.at[peer],
        dst_ref=recv.at[d],
        send_sem=send.at[d],
        recv_sem=got.at[d],
        device_id=ident(peer),
        device_id_type=MESH,
    )


def gram_sum_kernel(n, pair, count, *refs):
    rows_refs, (out_ref, gram, cross, part, recv, send, got, send2, got2) = refs[:count], refs[count:]
    me, size, ident = peers_of(n, pair)
    barrier = greet(me, size, ident)
    block = part.shape[1]
    width = gram.shape[0]
    gram[...] = jnp.zeros_like(gram)
    cross[...] = jnp.zeros_like(cross)

    def product(a, b):
        return lax.dot_general(
            a, b, (((0,), (0,)), ((), ())), preferred_element_type=jnp.float32
        )

    for rows_ref in rows_refs:
        step = math.gcd(rows_ref.shape[0], 512)

        def add(i, carry, rows_ref=rows_ref, step=step):
            rows = rows_ref[pl.ds(pl.multiple_of(i * step, step), step), :]
            high = rows.astype(jnp.bfloat16)
            rest = rows - high.astype(jnp.float32)
            middle = rest.astype(jnp.bfloat16)
            low = (rest - middle.astype(jnp.float32)).astype(jnp.bfloat16)
            wide = product(high, jnp.concatenate([high, middle], axis=1))
            gram[...] += wide[:, :width] + product(middle, middle)
            cross[...] += wide[:, width:] + product(high, low)
            return carry

        lax.fori_loop(0, rows_ref.shape[0] // step, add, 0)
    turned = cross[...]
    gram[...] += turned + turned.T
    for r in range(size):
        part[r] = gram[r * block : (r + 1) * block, :]
    pl.semaphore_wait(barrier, size - 1)
    copies = [send_block(part, recv, me, size, ident, send, got, d) for d in range(1, size)]
    for copy in copies:
        copy.start()
    total = part[me]
    for d in range(1, size):
        copies[d - 1].wait_recv()
        total = total + recv[d]
    out_ref[me] = total
    spread = []
    for d in range(1, size):
        spread.append(
            pltpu.make_async_remote_copy(
                src_ref=out_ref.at[me],
                dst_ref=out_ref.at[me],
                send_sem=send2.at[d],
                recv_sem=got2.at[d],
                device_id=ident(lax.rem(me + d, size)),
                device_id_type=MESH,
            )
        )
    for copy in spread:
        copy.start()
    for copy in spread:
        copy.wait_recv()
    for copy in copies + spread:
        copy.wait_send()


def gram_sum(parts, n, pair, ident):
    size = 2 * n if pair else n
    width = parts[0].shape[1]
    dtype = parts[0].dtype
    shape = (size, width // size, width)
    out = pl.pallas_call(
        functools.partial(gram_sum_kernel, n, pair, len(parts)),
        out_shape=jax.ShapeDtypeStruct(shape, dtype),
        in_specs=[VMEM] * len(parts),
        out_specs=VMEM,
        scratch_shapes=[
            pltpu.VMEM((width, width), dtype),
            pltpu.VMEM((width, width), dtype),
            pltpu.VMEM(shape, dtype),
            pltpu.VMEM(shape, dtype),
        ]
        + [pltpu.SemaphoreType.DMA((size,))] * 4,
        compiler_params=pltpu.CompilerParams(collective_id=ident, has_side_effects=True),
        name=f"gram_sum_{ident}",
    )(*parts)
    return out.reshape(width, width)


def score_kernel(
    n, scale, grow, centered_ref, own_ref, basis_ref, out_ref,
    held, narrow, part, recv, loaded, send, got, swap_send, swap_got,
):
    me, size, ident = peers_of(n, False)
    cohort = lax.axis_index("cohort")
    side = lax.rem(cohort, 2)
    partner = {"cohort": cohort + 1 - 2 * side}
    rows, half = held.shape[2:]
    order = [lax.rem(me + d, size) for d in list(range(1, size)) + [0]]
    loads = []
    for peer in order:
        pair = []
        for h in range(2):
            pair.append(
                pltpu.make_async_copy(
                    centered_ref.at[
                        pl.ds(pl.multiple_of(peer * rows, rows), rows), pl.ds(h * half, half)
                    ],
                    held.at[peer, h],
                    loaded.at[peer, h],
                )
            )
        loads.append(pair)
        for copy in pair:
            copy.start()
    barrier = greet(me, size, ident)
    pl.semaphore_signal(barrier, inc=1, device_id=partner, device_id_type=MESH)
    basis_ref[side] = own_ref[...]
    narrow[...] = own_ref[...].astype(jnp.bfloat16)
    pl.semaphore_wait(barrier, size)
    cross = pltpu.make_async_remote_copy(
        src_ref=own_ref,
        dst_ref=basis_ref.at[side],
        send_sem=swap_send,
        recv_sem=swap_got,
        device_id=partner,
        device_id_type=MESH,
    )
    cross.start()
    for peer, pair in zip(order, loads):
        for copy in pair:
            copy.wait()
        part[peer] = jnp.dot(held[peer, side], narrow[...], preferred_element_type=jnp.float32)
    cross.wait_recv()
    narrow[...] = basis_ref[1 - side].astype(jnp.bfloat16)
    copies = []
    for d, peer in zip(list(range(1, size)) + [0], order):
        part[peer] = part[peer] + jnp.dot(
            held[peer, 1 - side], narrow[...], preferred_element_type=jnp.float32
        )
        if d:
            copies.append(send_block(part, recv, me, size, ident, send, got, d))
            copies[-1].start()
    basis_ref[...] = basis_ref[...] * grow
    total = part[me]
    for d in range(1, size):
        copies[d - 1].wait_recv()
        total = total + recv[d]
    out_ref[...] = total * scale
    cross.wait_send()
    for copy in copies:
        copy.wait_send()


def basis_and_scores(centered, own, n, scale, grow, ident):
    subjects = centered.shape[0]
    half, width = own.shape
    rows = subjects // n
    blocks = (n, rows, width)
    basis, scores = pl.pallas_call(
        functools.partial(score_kernel, n, scale, grow),
        out_shape=(
            jax.ShapeDtypeStruct((2, half, width), own.dtype),
            jax.ShapeDtypeStruct((rows, width), jnp.float32),
        ),
        in_specs=[pl.BlockSpec(memory_space=pl.ANY), VMEM],
        out_specs=(VMEM, VMEM),
        scratch_shapes=[
            pltpu.VMEM((n, 2, rows, half), centered.dtype),
            pltpu.VMEM((half, width), jnp.bfloat16),
            pltpu.VMEM(blocks, jnp.float32),
            pltpu.VMEM(blocks, jnp.float32),
            pltpu.SemaphoreType.DMA((n, 2)),
            pltpu.SemaphoreType.DMA((n,)),
            pltpu.SemaphoreType.DMA((n,)),
            pltpu.SemaphoreType.DMA,
            pltpu.SemaphoreType.DMA,
        ],
        compiler_params=pltpu.CompilerParams(collective_id=ident, has_side_effects=True),
        name="basis_and_scores",
    )(centered, own)
    return basis.reshape(2 * half, width), scores


def inverse_of(g_ref, x_ref):
    size = g_ref.shape[0]
    step = 8
    tiles = size // step
    lane = lax.broadcasted_iota(jnp.int32, (step, size), 1)
    sub = lax.broadcasted_iota(jnp.int32, (step, size), 0)

    def full(x):
        return jnp.broadcast_to(x, (step, size))

    def total(terms):
        while len(terms) > 1:
            terms = [terms[i] + terms[i + 1] for i in range(0, len(terms), 2)]
        return terms[0]

    left = [g_ref[t * step : (t + 1) * step, :] for t in range(tiles)]
    right = [(lane == sub + t * step).astype(jnp.float32) for t in range(tiles)]
    for t in range(tiles):
        at = t * step
        cols = [full(left[t][:, at + k : at + k + 1]) for k in range(step)]
        e = [[full(cols[k][i : i + 1, :]) for k in range(i + 1)] for i in range(step)]
        rows = [full(left[t][i : i + 1, :]) for i in range(step)]
        rows_x = [full(right[t][i : i + 1, :]) for i in range(step)]
        f = {}
        inv = []
        for s in range(step):
            inv.append(1.0 / e[s][s])
            for i in range(s + 1, step):
                f[i, s] = e[i][s] * inv[s]
                for k in range(s + 1, i + 1):
                    e[i][k] = e[i][k] - f[i, s] * e[k][s]
            for i in range(s + 1, step):
                rows[i] = rows[i] - f[i, s] * rows[s]
                rows_x[i] = rows_x[i] - f[i, s] * rows_x[s]
        out = rows_x[0] * lax.rsqrt(e[0][0])
        for s in range(1, step):
            out = jnp.where(sub == s, rows_x[s] * lax.rsqrt(e[s][s]), out)
        x_ref[at : at + step, :] = out
        rows = [rows[s] * inv[s] for s in range(step)]
        rows_x = [rows_x[s] * inv[s] for s in range(step)]
        for u in range(t + 1, tiles):
            c = [full(left[u][:, at + s : at + s + 1]) for s in range(step)]
            for s in range(step):
                for r in range(s):
                    c[s] = c[s] - f[s, r] * c[r]
            left[u] = left[u] - total([c[s] * rows[s] for s in range(step)])
            right[u] = right[u] - total([c[s] * rows_x[s] for s in range(step)])


def map_kernel(g_ref, mix_ref, out_ref, x_ref):
    inverse_of(g_ref, x_ref)
    out_ref[...] = lax.dot_general(
        x_ref[...],
        mix_ref[...],
        (((0,), (0,)), ((), ())),
        precision=HIGHEST,
        preferred_element_type=jnp.float32,
    )


def lower_inverse(gram):
    return pl.pallas_call(
        inverse_of,
        out_shape=jax.ShapeDtypeStruct(gram.shape, gram.dtype),
        in_specs=[VMEM],
        out_specs=VMEM,
        name="lower_inverse",
    )(gram)


def mixing_map(gram, mix):
    return pl.pallas_call(
        map_kernel,
        out_shape=jax.ShapeDtypeStruct(gram.shape, gram.dtype),
        in_specs=[VMEM, VMEM],
        out_specs=VMEM,
        scratch_shapes=[pltpu.VMEM(gram.shape, gram.dtype)],
        name="mixing_map",
    )(gram, mix)


def sketch_kernel(steps, side_ref, shapes_ref, signs_ref, centered_ref, mine_ref, given_ref, turned):
    i = pl.program_id(0)

    @pl.when(i == 0)
    def _():
        turned[...] = signs_ref[...].astype(jnp.float32).T.astype(jnp.bfloat16)

    data = shapes_ref[...].astype(jnp.float32)
    mean = jnp.sum(data, axis=0, keepdims=True) * (1.0 / data.shape[0])
    centered = (data - mean).astype(jnp.bfloat16)
    centered_ref[...] = centered
    sketch = jnp.dot(turned[...], centered, preferred_element_type=jnp.float32).T

    @pl.when(i < steps)
    def _():
        mine_ref[...] = sketch

    @pl.when(i >= steps)
    def _():
        given_ref[...] = sketch


def center_and_sketch(side, shapes, signs):
    subjects, coords = shapes.shape
    width = signs.shape[1]
    half = coords // 2
    tile = math.gcd(half, 2048)
    steps = half // tile

    def column(i, side):
        kept = i < steps
        return jnp.where(kept, side[0] * steps + i, (1 - side[0]) * steps + i - steps)

    return pl.pallas_call(
        functools.partial(sketch_kernel, steps),
        grid_spec=pltpu.PrefetchScalarGridSpec(
            num_scalar_prefetch=1,
            grid=(2 * steps,),
            in_specs=[
                pl.BlockSpec((subjects, tile), lambda i, side: (0, column(i, side))),
                pl.BlockSpec((subjects, width), lambda i, side: (0, 0)),
            ],
            out_specs=(
                pl.BlockSpec((subjects, tile), lambda i, side: (0, column(i, side))),
                pl.BlockSpec((tile, width), lambda i, side: (jnp.minimum(i, steps - 1), 0)),
                pl.BlockSpec((tile, width), lambda i, side: (jnp.maximum(i - steps, 0), 0)),
            ),
            scratch_shapes=[pltpu.VMEM((width, subjects), jnp.bfloat16)],
        ),
        out_shape=(
            jax.ShapeDtypeStruct((subjects, coords), jnp.bfloat16),
            jax.ShapeDtypeStruct((half, width), jnp.float32),
            jax.ShapeDtypeStruct((half, width), jnp.float32),
        ),
        name="center_and_sketch",
    )(side.reshape(1), shapes, signs)


def times_t(a, b):
    return lax.dot_general(a, b, (((1,), (1,)), ((), ())), precision=HIGHEST)


def mix(own, own_map, other, other_map):
    return jnp.matmul(own, own_map, precision=HIGHEST) + jnp.matmul(
        other, other_map, precision=HIGHEST
    )


def swap(value, distance):
    size = lax.axis_size("cohort")
    return lax.ppermute(value, "cohort", [(i, i ^ distance) for i in range(size)])


def on_device(shapes, sketch_signs, merge_sketch):
    n = lax.axis_size("coord")
    position = lax.axis_index("cohort")
    side = position % 2
    upper = position // 2 % 2
    centered, mine, given = center_and_sketch(side, shapes[0], sketch_signs[0])

    theirs = swap(given, 1)
    own_map = mixing_map(gram_sum((mine, given), n, False, 0), merge_sketch[0][side])
    mine = mix(mine, own_map, theirs, swap(own_map, 1))

    theirs = swap(mine, 2)
    own_map = mixing_map(gram_sum((mine,), n, True, 1), merge_sketch[1][upper])
    mine = mix(mine, own_map, theirs, swap(own_map, 2))

    mine = times_t(mine, lower_inverse(gram_sum((mine,), n, True, 2)))
    width = mine.shape[1]
    total_coords = shapes.shape[2] * n
    basis, scores = basis_and_scores(
        centered, mine, n, 4.0 * math.sqrt(width / total_coords), math.sqrt(total_coords), 3
    )
    return basis[None], scores[None]


def solution(mesh):
    placed = (P("cohort", None, "coord"), P("cohort", None, None), P())
    return jax.shard_map(
        on_device,
        mesh=mesh,
        in_specs=placed,
        out_specs=(P("cohort", "coord", None), P("cohort", "coord", None)),
        check_vma=False,
    )
```

profile of v0, /device:TPU:0, one launch (start us, length us, event | category | flops | bytes accessed | tf_op | source)
XLA Modules:
  0.0 111.6 jit_solution(494960051169775755)
XLA Ops:
  0.6 0.0 copy-start.1
  0.7 9.6 %center_and_sketch.1 = (bf16[1024,4096]{1,0:T(8,128)(2,1)}, f32[2048,128]{1,0:T(8,128)}, f32[2048,128]{1,0:T(8,128)}) custom-call(s32[1]{0:T(128)} %bitcast.side_ref, bf16[1024,4096]{1,0:T(8,128)(2,1)} %bitcast.22, s32[1024,128]{1,0:T(8,128)} %bitcast.24), custom_call_target="tpu_custom_call" | custom-call | tf_op jit(solution)/shard_map/center_and_sketch/pallas_call | solution.py:343
  10.3 0.5 collective-permute-start
  10.7 16.5 %gram_sum_0.1 = f32[8,16,128]{2,1,0:T(8,128)} custom-call(f32[2048,128]{1,0:T(8,128)} %get-tuple-element.8.refs_0_, f32[2048,128]{1,0:T(8,128)} %get-tuple-element.9.refs_1_), custom_call_target="tpu_custom_call" | custom-call | tf_op jit(solution)/shard_map/gram_sum_0/pallas_call | solution.py:116
  27.3 0.0 copy-done.1
  27.3 0.6 dynamic-slice_bitcast_fusion.1.mix_ref
  27.9 6.1 %mixing_map.2 = f32[128,128]{1,0:T(8,128)} custom-call(f32[128,128]{1,0:T(8,128)} %bitcast.25, f32[128,128]{1,0:T(8,128)} %dynamic-slice_bitcast_fusion.1.mix_ref), custom_call_target="tpu_custom_call" | custom-call | tf_op jit(solution)/shard_map/mixing_map/pallas_call | solution.py:300
  34.0 0.0 collective-permute-start.1
  34.0 2.2 %fusion.1 = f32[2048,128]{1,0:T(8,128)S(1)} fusion(f32[2048,128]{1,0:T(8,128)} %get-tuple-element.8.refs_0_, f32[128,128]{1,0:T(8,128)} %mixing_map.2), kind=kOutput, calls=%fused_computation.5 | convolution fusion | flops 402653184 | bytes 2162688 | tf_op jit(solution)/shard_map/dot_general | solution.py:373
  36.2 0.0 collective-permute-done.1
  36.2 0.0 collective-permute-done
  36.3 1.0 convolution_add_fusion.1.refs_0_
  37.2 0.0 copy-start
  37.2 1.6 %collective-permute-start.2 = (f32[2048,128]{1,0:T(8,128)S(1)}, f32[2048,128]{1,0:T(8,128)S(1)}, u32[]{:S(2)}, u32[]{:S(2)}) collective-permute-start(f32[2048,128]{1,0:T(8,128)S(1)} %convolution_add_fusion.1.refs_0_), channel_id=1, source_target_pairs={{0,2},{1,3},{2,0},{3,1},{4,6},{5,7},{6,4},{7,5},{8,10},{9,11},{10,... | collective-permute-start | bytes 3145736 | tf_op jit(solution)/shard_map/ppermute | solution.py:380
  38.8 0.6 dynamic-slice_bitcast_fusion.mix_ref
  39.4 0.0 copy-done
  39.4 13.4 %gram_sum_1.1 = f32[16,8,128]{2,1,0:T(8,128)} custom-call(f32[2048,128]{1,0:T(8,128)} %copy-done), custom_call_target="tpu_custom_call" | custom-call | tf_op jit(solution)/shard_map/gram_sum_1/pallas_call | solution.py:116
  52.9 6.1 %mixing_map.3 = f32[128,128]{1,0:T(8,128)} custom-call(f32[128,128]{1,0:T(8,128)} %bitcast.26, f32[128,128]{1,0:T(8,128)} %dynamic-slice_bitcast_fusion.mix_ref), custom_call_target="tpu_custom_call" | custom-call | tf_op jit(solution)/shard_map/mixing_map/pallas_call | solution.py:300
  58.9 0.5 collective-permute-start.3
  59.5 2.2 %fusion.2 = f32[2048,128]{1,0:T(8,128)S(1)} fusion(f32[2048,128]{1,0:T(8,128)} %copy-done, f32[128,128]{1,0:T(8,128)} %mixing_map.3), kind=kOutput, calls=%fused_computation.6 | convolution fusion | flops 402653184 | bytes 2162688 | tf_op jit(solution)/shard_map/dot_general | solution.py:373
  61.7 2.6 %collective-permute-done.3 = f32[128,128]{1,0:T(8,128)S(1)} collective-permute-done((f32[128,128]{1,0:T(8,128)}, f32[128,128]{1,0:T(8,128)S(1)}, u32[]{:S(2)}, u32[]{:S(2)}) %collective-permute-start.3) | collective-permute-done | bytes 65568 | tf_op jit(solution)/shard_map/ppermute | solution.py:380
  64.3 0.0 collective-permute-done.2
  64.3 1.9 %convolution_add_fusion.refs_0_ = f32[2048,128]{1,0:T(8,128)} fusion(f32[2048,128]{1,0:T(8,128)S(1)} %fusion.2, f32[2048,128]{1,0:T(8,128)S(1)} %collective-permute-done.2, f32[128,128]{1,0:T(8,128)S(1)} %collective-permute-done.3), kind=kOutput, calls=%fused_computation | convolution fusion | flops 402915328 | bytes 3211264 | tf_op jit(solution)/shard_map/dot_general | solution.py:373
  66.2 13.4 %gram_sum_2.1 = f32[16,8,128]{2,1,0:T(8,128)} custom-call(f32[2048,128]{1,0:T(8,128)} %convolution_add_fusion.refs_0_), custom_call_target="tpu_custom_call" | custom-call | tf_op jit(solution)/shard_map/gram_sum_2/pallas_call | solution.py:116
  79.6 5.7 %lower_inverse.1 = f32[128,128]{1,0:T(8,128)} custom-call(f32[128,128]{1,0:T(8,128)} %bitcast.27), custom_call_target="tpu_custom_call" | custom-call | tf_op jit(solution)/shard_map/lower_inverse/pallas_call | solution.py:290
  85.3 3.2 %fusion.3.own_ref = f32[2048,128]{1,0:T(8,128)} fusion(f32[2048,128]{1,0:T(8,128)} %convolution_add_fusion.refs_0_, f32[128,128]{1,0:T(8,128)} %lower_inverse.1), kind=kOutput, calls=%fused_computation.7 | convolution fusion | flops 402653184 | bytes 2162688 | tf_op jit(solution)/shard_map/dot_general | solution.py:369
  88.5 18.5 %basis_and_scores.1 = (f32[2,2048,128]{2,1,0:T(8,128)}, f32[128,128]{1,0:T(8,128)}) custom-call(bf16[1024,4096]{1,0:T(8,128)(2,1)} %get-tuple-element.7.centered_ref, f32[2048,128]{1,0:T(8,128)} %fusion.3.own_ref), custom_call_target="tpu_custom_call" | custom-call | tf_op jit(solution)/shard_map/basis_and_scores/pallas_call | solution.py:204
  107.0 3.0 %copy.7 = f32[1,4096,128]{2,1,0:T(8,128)} copy(f32[1,4096,128]{2,1,0:T(8,128)} %bitcast.23) | data formatting | bytes 4194304
  110.1 1.5 %copy.8 = f32[1,128,128]{2,1,0:T(8,128)} copy(f32[1,128,128]{2,1,0:T(8,128)} %bitcast.28) | data formatting | bytes 131072
  (1 shorter events, 0.0 us)
Async XLA Ops:
  0.6 26.6 %copy-start.1 = (f32[2,2,128,128]{3,2,1,0:T(8,128)S(1)}, f32[2,2,128,128]{3,2,1,0:T(8,128)}, u32[]{:S(2)}) copy-start(f32[2,2,128,128]{3,2,1,0:T(8,128)} %param.5) | copy-start | bytes 786436
  10.3 26.0 %collective-permute-start = (f32[2048,128]{1,0:T(8,128)}, f32[2048,128]{1,0:T(8,128)S(1)}, u32[]{:S(2)}, u32[]{:S(2)}) collective-permute-start(f32[2048,128]{1,0:T(8,128)} %get-tuple-element.9.refs_1_), channel_id=1, source_target_pairs={{0,1},{1,0},{2,3},{3,2},{4,5},{5,4},{6,7},{7,6},{8,9},{9,8},{10,11... | collective-permute-start | bytes 3145736 | tf_op jit(solution)/shard_map/ppermute | solution.py:380
  34.0 2.2 %collective-permute-start.1 = (f32[128,128]{1,0:T(8,128)}, f32[128,128]{1,0:T(8,128)S(1)}, u32[]{:S(2)}, u32[]{:S(2)}) collective-permute-start(f32[128,128]{1,0:T(8,128)} %mixing_map.2), channel_id=1, source_target_pairs={{0,1},{1,0},{2,3},{3,2},{4,5},{5,4},{6,7},{7,6},{8,9},{9,8},{10,11... | collective-permute-start | bytes 196616 | tf_op jit(solution)/shard_map/ppermute | solution.py:380
  37.2 2.2 %copy-start = (f32[2048,128]{1,0:T(8,128)}, f32[2048,128]{1,0:T(8,128)S(1)}, u32[]{:S(2)}) copy-start(f32[2048,128]{1,0:T(8,128)S(1)} %convolution_add_fusion.1.refs_0_) | copy-start | bytes 3145732
  37.2 27.0 %collective-permute-start.2 = (f32[2048,128]{1,0:T(8,128)S(1)}, f32[2048,128]{1,0:T(8,128)S(1)}, u32[]{:S(2)}, u32[]{:S(2)}) collective-permute-start(f32[2048,128]{1,0:T(8,128)S(1)} %convolution_add_fusion.1.refs_0_), channel_id=1, source_target_pairs={{0,2},{1,3},{2,0},{3,1},{4,6},{5,7},{6,4},{7,5},{8,10},{9,11},{10,... | collective-permute-start | bytes 3145736 | tf_op jit(solution)/shard_map/ppermute | solution.py:380
  58.9 5.3 %collective-permute-start.3 = (f32[128,128]{1,0:T(8,128)}, f32[128,128]{1,0:T(8,128)S(1)}, u32[]{:S(2)}, u32[]{:S(2)}) collective-permute-start(f32[128,128]{1,0:T(8,128)} %mixing_map.3), channel_id=1, source_target_pairs={{0,2},{1,3},{2,0},{3,1},{4,6},{5,7},{6,4},{7,5},{8,10},{9,11},{10,... | collective-permute-start | bytes 196616 | tf_op jit(solution)/shard_map/ppermute | solution.py:380
where the time goes:
time: 113 us; the launch traced here: 112 us
  Pallas kernels  89.3 us (79%)
  matrix products  10.5 us (9%)
  local copies, waits for them, and re-layouts  5.82 us (5%)
  waiting for transfers between devices  2.61 us (2%)
  starting transfers between devices  2.54 us (2%)
    pallas_call x3, Pallas kernels, gram_sum(): pl.pallas_call(functools.partial(gram_sum_kernel, n, pair, len(parts)), o...  43.3 us
    pallas_call x1, Pallas kernels, basis_and_scores(): pl.pallas_call(functools.partial(score_kernel, n, scale, grow), out_shape...  18.5 us
    pallas_call x2, Pallas kernels, mixing_map(): pl.pallas_call(map_kernel, out_shape=jax.ShapeDtypeStruct(gram.shape, gra...  12.2 us
    pallas_call x1, Pallas kernels, center_and_sketch(): pl.pallas_call(functools.partial(sketch_kernel, steps), grid_spec=pltpu.P...  9.64 us
    pallas_call x1, Pallas kernels, lower_inverse(): pl.pallas_call(inverse_of, out_shape=jax.ShapeDtypeStruct(gram.shape, gra...  5.68 us
    unnamed x6, local copies, waits for them, and re-layouts  4.53 us
    dot_general x2, matrix products, mix(): jnp.matmul(own, own_map, precision=HIGHEST)  4.39 us
    dot_general x1, matrix products, times_t(): return lax.dot_general(a, b, (((1,), (1,)), ((), ())), precision=HIGHEST)  3.19 us
  transfers between devices with their start and end apart: 4, of which 1 were waited for; matrix products, arithmetic and copies ran while one was open for 5% of the time, Pallas kernels for 38%

commit v1 on v0

v1 whole, which is shorter than its diff:
```python
import functools
import math

import jax
import jax.numpy as jnp
from jax import lax
from jax.experimental import pallas as pl
from jax.experimental.pallas import tpu as pltpu
from jax.sharding import PartitionSpec as P

HIGHEST = lax.Precision.HIGHEST
MESH = pl.DeviceIdType.MESH
F32 = jnp.float32
BF16 = jnp.bfloat16


def dot(a, b):
    return jnp.dot(a, b, preferred_element_type=F32)


def dot_high(a, b, dims):
    return lax.dot_general(a, b, (dims, ((), ())), precision=HIGHEST, preferred_element_type=F32)


def split(x):
    high = x.astype(BF16)
    return high, (x - high.astype(F32)).astype(BF16)


def cross_product(a, b):
    dims = (((0,), (0,)), ((), ()))
    a_high, a_mid = split(a)
    b_high, b_mid = split(b)
    wide = lax.dot_general(
        a_high, jnp.concatenate([b_high, b_mid], axis=1), dims, preferred_element_type=F32
    )
    width = b.shape[1]
    return (
        wide[:, :width]
        + wide[:, width:]
        + lax.dot_general(a_mid, b_high, dims, preferred_element_type=F32)
    )


def stack_map(stacked, which, value):
    high, mid = split(value)
    width = value.shape[0]
    base = 3 * width * which
    stacked[base : base + width, :] = high
    stacked[base + width : base + 2 * width, :] = high
    stacked[base + 2 * width : base + 3 * width, :] = mid


def mix_rows(low, up, stacked):
    low_high, low_mid = split(low)
    up_high, up_mid = split(up)
    rows = jnp.concatenate([low_high, low_mid, low_high, up_high, up_mid, up_high], axis=1)
    return dot(rows, stacked[...])


def inverse_of(gram, x_ref):
    size = gram.shape[1]
    step = 8
    tiles = size // step
    lane = lax.broadcasted_iota(jnp.int32, (step, size), 1)
    sub = lax.broadcasted_iota(jnp.int32, (step, size), 0)

    def full(x):
        return jnp.broadcast_to(x, (step, size))

    def total(terms):
        while len(terms) > 1:
            terms = [terms[i] + terms[i + 1] for i in range(0, len(terms), 2)]
        return terms[0]

    left = gram.reshape(tiles, step, size)
    right = jnp.stack([(lane == sub + t * step).astype(F32) for t in range(tiles)])
    for t in range(tiles):
        at = t * step
        head, head_x = left[0], right[0]
        cols = [full(head[:, at + k : at + k + 1]) for k in range(step)]
        e = [[full(cols[k][i : i + 1, :]) for k in range(i + 1)] for i in range(step)]
        rows = [full(head[i : i + 1, :]) for i in range(step)]
        rows_x = [full(head_x[i : i + 1, :]) for i in range(step)]
        f = {}
        inv = []
        for s in range(step):
            inv.append(1.0 / e[s][s])
            for i in range(s + 1, step):
                f[i, s] = e[i][s] * inv[s]
                for k in range(s + 1, i + 1):
                    e[i][k] = e[i][k] - f[i, s] * e[k][s]
            for i in range(s + 1, step):
                rows[i] = rows[i] - f[i, s] * rows[s]
                rows_x[i] = rows_x[i] - f[i, s] * rows_x[s]
        out = rows_x[0] * lax.rsqrt(e[0][0])
        for s in range(1, step):
            out = jnp.where(sub == s, rows_x[s] * lax.rsqrt(e[s][s]), out)
        x_ref[at : at + step, :] = out
        if t + 1 == tiles:
            break
        rows = [rows[s] * inv[s] for s in range(step)]
        rows_x = [rows_x[s] * inv[s] for s in range(step)]
        for s in range(step - 2, -1, -1):
            for i in range(s + 1, step):
                rows[s] = rows[s] - f[i, s] * rows[i]
                rows_x[s] = rows_x[s] - f[i, s] * rows_x[i]
        left, right = left[1:], right[1:]
        c = [jnp.broadcast_to(left[:, :, at + s : at + s + 1], left.shape) for s in range(step)]
        left = left - total([c[s] * rows[s][None] for s in range(step)])
        right = right - total([c[s] * rows_x[s][None] for s in range(step)])


def remote(src, dst, send, got, device):
    return pltpu.make_async_remote_copy(
        src_ref=src, dst_ref=dst, send_sem=send, recv_sem=got, device_id=device, device_id_type=MESH
    )


def scatter(part, recv, group, send, got):
    me, size, ident = group
    copies = []
    for d in range(1, size):
        peer = lax.rem(me + d, size)
        copies.append(remote(part.at[peer], recv.at[d], send.at[d], got.at[d], ident(peer)))
    return copies


def start(copies):
    for copy in copies:
        copy.start()


def summed(part, recv, group, copies):
    me, size, ident = group
    total = part[me]
    for d in range(1, size):
        copies[d - 1].wait_recv()
        total = total + recv[d]
    return total


def spread(out, group, send, got):
    me, size, ident = group
    return [
        remote(out.at[me], out.at[me], send.at[d], got.at[d], ident(lax.rem(me + d, size)))
        for d in range(1, size)
    ]


def received(copies):
    for copy in copies:
        copy.wait_recv()


def sent(copies):
    for copy in copies:
        copy.wait_send()


def whole_kernel(
    n, tile, shapes_ref, signs_ref, merge_ref, basis_ref, scores_ref,
    held, signs, merge, turned, given, pairs, mixed, stacked, maps, outer, x_ref, narrow,
    wide, products, gram_part, gram_recv, gram, low_part, low_recv, low_gram,
    up_part, up_recv, up_gram, up_other, score_part, score_recv,
    loaded, small, give_send, give_got, gram_send, gram_got, gram_send2, gram_got2,
    low_send, low_got, low_send2, low_got2, up_send, up_got, up_send2, up_got2,
    cross_send, cross_got, basis_send, basis_got, score_send, score_got, map_send, map_got,
):
    coord = lax.axis_index("coord")
    cohort = lax.axis_index("cohort")
    side = lax.rem(cohort, 2)
    upper = lax.rem(cohort // 2, 2)
    base = cohort - side
    partner = {"cohort": cohort + 1 - 2 * side}
    across = {"cohort": cohort + 2 - 4 * upper}
    line = (coord, n, lambda r: {"coord": r})
    pair = (
        coord * 2 + side, 2 * n, lambda r: {"coord": r // 2, "cohort": base + lax.rem(r, 2)}
    )
    chunks = held.shape[0] // 2
    half = chunks * tile
    width = turned.shape[0]

    def rows_of(c):
        return pl.ds(pl.multiple_of(c * tile, tile), tile)

    small_copies = [
        pltpu.make_async_copy(signs_ref, signs, small.at[0]),
        pltpu.make_async_copy(merge_ref, merge, small.at[1]),
    ]
    start(small_copies)

    def load(h, c):
        at = pl.multiple_of((h * chunks + c) * tile, tile)
        return pltpu.make_async_copy(
            shapes_ref.at[:, pl.ds(at, tile)], held.at[h * chunks + c], loaded.at[h, c]
        )

    for h in (1 - side, side):
        for c in range(chunks):
            load(h, c).start()

    barrier = pltpu.get_barrier_semaphore()
    me, size, ident = pair
    for d in range(1, size):
        pl.semaphore_signal(
            barrier, inc=1, device_id=ident(lax.rem(me + d, size)), device_id_type=MESH
        )
    pl.semaphore_signal(barrier, inc=1, device_id=across, device_id_type=MESH)
    for copy in small_copies:
        copy.wait()
    turned[...] = signs[...].astype(F32).T.astype(BF16)
    for l in range(2):
        outer[l] = dot_high(merge[l, 0], merge[l, 0], ((0,), (0,))) + dot_high(
            merge[l, 1], merge[l, 1], ((0,), (0,))
        )
    wide[...] = jnp.zeros_like(wide)
    pl.semaphore_wait(barrier, size)

    def give(c):
        return remote(
            given.at[rows_of(c)], pairs.at[side, rows_of(c)], give_send.at[c], give_got.at[c], partner
        )

    def sketch(h, c):
        load(h, c).wait()
        block = held.at[h * chunks + c]
        mean = jnp.sum(block[...].astype(F32), axis=0, keepdims=True) * (1.0 / block.shape[0])
        block[...] = (block[...].astype(F32) - mean).astype(BF16)
        flat = dot(turned[...], block[...])
        rows = flat.T
        high, mid = split(rows)
        wide[...] += dot(flat.astype(BF16), jnp.concatenate([high, mid], axis=1))
        return rows

    def first(c, carry):
        given[rows_of(c)] = sketch(1 - side, c)
        give(c).start()
        return carry

    def second(c, carry):
        pairs[side, rows_of(c)] = sketch(side, c)
        return carry

    lax.fori_loop(0, chunks, first, 0)
    lax.fori_loop(0, chunks, second, 0)
    turn = wide[:, width:]
    own = wide[:, :width] + turn + turn.T
    gram_part[...] = own.reshape(gram_part.shape)
    copies = scatter(gram_part, gram_recv, line, gram_send, gram_got)
    start(copies)

    products[...] = jnp.zeros_like(products)

    def cross(c, carry):
        give(c).wait_recv()
        products[...] += cross_product(pairs[0, rows_of(c)], pairs[1, rows_of(c)])
        return carry

    lax.fori_loop(0, chunks, cross, 0)
    low_part[...] = products[...].reshape(low_part.shape)
    gram[coord] = summed(gram_part, gram_recv, line, copies)
    gathered = spread(gram, line, gram_send2, gram_got2)
    start(gathered)
    low_copies = scatter(low_part, low_recv, pair, low_send, low_got)
    start(low_copies)
    received(gathered)

    inverse_of(gram[...].reshape(width, width), x_ref)
    maps[0, side] = dot_high(x_ref[...], merge[0, side], ((0,), (0,)))
    map_swap = remote(maps.at[0, side], maps.at[0, side], map_send.at[0], map_got.at[0], partner)
    map_swap.start()
    low_gram[pair[0]] = summed(low_part, low_recv, pair, low_copies)
    low_gathered = spread(low_gram, pair, low_send2, low_got2)
    start(low_gathered)
    map_swap.wait_recv()
    for i in range(2):
        stack_map(stacked, i, maps[0, i])

    def ship(c):
        return remote(
            mixed.at[upper, rows_of(c)], mixed.at[upper, rows_of(c)],
            cross_send.at[c], cross_got.at[c], across,
        )

    def turn_of(which, i):
        return lax.rem(i + which * (chunks // 2), chunks)

    def blend(i, carry):
        c = turn_of(upper, i)
        mixed[upper, rows_of(c)] = mix_rows(pairs[0, rows_of(c)], pairs[1, rows_of(c)], stacked)
        ship(c).start()
        return carry

    lax.fori_loop(0, chunks, blend, 0)
    received(low_gathered)
    inner = dot_high(
        maps[0, 0],
        dot_high(low_gram[...].reshape(width, width), maps[0, 1], ((1,), (0,))),
        ((0,), (0,)),
    )
    inverse_of(outer[0] + inner + inner.T, x_ref)
    maps[1, upper] = dot_high(x_ref[...], merge[1, upper], ((0,), (0,)))
    across_swap = remote(maps.at[1, upper], maps.at[1, upper], map_send.at[1], map_got.at[1], across)
    across_swap.start()

    products[...] = jnp.zeros_like(products)

    def meet(i, carry):
        c = turn_of(1 - upper, i)
        ship(c).wait_recv()
        products[...] += cross_product(mixed[0, rows_of(c)], mixed[1, rows_of(c)])
        return carry

    lax.fori_loop(0, chunks // 2, meet, 0)
    up_part[...] = products[...].reshape(up_part.shape)
    up_copies = scatter(up_part, up_recv, pair, up_send, up_got)
    start(up_copies)
    up_other[upper] = summed(up_part, up_recv, pair, up_copies)
    up_swap = remote(up_other.at[upper], up_other.at[upper], map_send.at[2], map_got.at[2], across)
    up_swap.start()
    up_swap.wait_recv()
    up_gram[pair[0]] = up_other[0] + up_other[1]
    up_gathered = spread(up_gram, pair, up_send2, up_got2)
    start(up_gathered)
    across_swap.wait_recv()
    received(up_gathered)
    inner = dot_high(
        maps[1, 0],
        dot_high(up_gram[...].reshape(width, width), maps[1, 1], ((1,), (0,))),
        ((0,), (0,)),
    )
    inverse_of(outer[1] + inner + inner.T, x_ref)
    for i in range(2):
        stack_map(stacked, i, dot_high(maps[1, i], x_ref[...], ((1,), (1,))))

    def hand(c):
        return remote(
            basis_ref.at[side, rows_of(c)], basis_ref.at[side, rows_of(c)],
            basis_send.at[c], basis_got.at[c], partner,
        )

    def finish(c):
        rows = mix_rows(mixed[0, rows_of(c)], mixed[1, rows_of(c)], stacked)
        basis_ref[side, rows_of(c)] = rows
        narrow[side * chunks + c] = rows.astype(BF16)
        hand(c).start()


    def arriving(i, carry):
        c = turn_of(1 - upper, i)
        ship(c).wait_recv()
        finish(c)
        return carry

    def local(i, carry):
        finish(turn_of(1 - upper, i))
        return carry

    lax.fori_loop(0, chunks // 2, local, 0)
    lax.fori_loop(chunks // 2, chunks, arriving, 0)

    block = score_part.shape[1]
    order = [lax.rem(coord + d, n) for d in list(range(1, n)) + [0]]

    def taken(peer, h):
        rows = pl.ds(pl.multiple_of(peer * block, block), block)
        total = dot(held[h * chunks, rows], narrow[h * chunks])
        for c in range(1, chunks):
            total = total + dot(held[h * chunks + c, rows], narrow[h * chunks + c])
        return total

    for peer in order:
        score_part[peer] = taken(peer, side)
    for c in range(chunks):
        hand(c).wait_recv()
        narrow[(1 - side) * chunks + c] = basis_ref[1 - side, rows_of(c)].astype(BF16)
    score_copies = scatter(score_part, score_recv, line, score_send, score_got)
    for d, peer in zip(list(range(1, n)) + [0], order):
        score_part[peer] = score_part[peer] + taken(peer, 1 - side)
        if d:
            score_copies[d - 1].start()
    scores_ref[...] = summed(score_part, score_recv, line, score_copies)

    sent(copies + gathered + low_copies + low_gathered + up_copies + up_gathered + score_copies)
    sent([map_swap, across_swap, up_swap])
    for c in range(chunks):
        give(c).wait_send()
        ship(c).wait_send()
        hand(c).wait_send()


def on_device(shapes, sketch_signs, merge_sketch):
    n = lax.axis_size("coord")
    _, subjects, coords = shapes.shape
    width = sketch_signs.shape[2]
    half = coords // 2
    tile = math.gcd(half // 2, 512)
    chunks = half // tile
    rows = subjects // n
    line = (n, width // n, width)
    pair = (2 * n, width // (2 * n), width)
    vmem, dma = pltpu.VMEM, pltpu.SemaphoreType.DMA
    basis, scores = pl.pallas_call(
        functools.partial(whole_kernel, n, tile),
        out_shape=(
            jax.ShapeDtypeStruct((2, half, width), F32),
            jax.ShapeDtypeStruct((rows, width), F32),
        ),
        in_specs=[pl.BlockSpec(memory_space=pl.ANY)] * 3,
        out_specs=(pl.BlockSpec(memory_space=vmem), pl.BlockSpec(memory_space=vmem)),
        scratch_shapes=[
            vmem((2 * chunks, subjects, tile), BF16),
            vmem((subjects, width), jnp.int32),
            vmem(merge_sketch.shape, F32),
            vmem((width, subjects), BF16),
            vmem((half, width), F32),
            vmem((2, half, width), F32),
            vmem((2, half, width), F32),
            vmem((6 * width, width), BF16),
            vmem((2, 2, width, width), F32),
            vmem((2, width, width), F32),
            vmem((width, width), F32),
            vmem((2 * chunks, tile, width), BF16),
            vmem((width, 2 * width), F32),
            vmem((width, width), F32),
            vmem(line, F32),
            vmem(line, F32),
            vmem(line, F32),
            vmem(pair, F32),
            vmem(pair, F32),
            vmem(pair, F32),
            vmem(pair, F32),
            vmem(pair, F32),
            vmem(pair, F32),
            vmem((2,) + pair[1:], F32),
            vmem((n, rows, width), F32),
            vmem((n, rows, width), F32),
            dma((2, chunks)),
            dma((2,)),
            dma((chunks,)),
            dma((chunks,)),
        ]
        + [dma((n,))] * 4
        + [dma((2 * n,))] * 8
        + [dma((chunks,))] * 4
        + [dma((n,))] * 2
        + [dma((3,))] * 2,
        compiler_params=pltpu.CompilerParams(
            collective_id=0, has_side_effects=True, vmem_limit_bytes=48 * 1024 * 1024
        ),
        name="shape_pca",
    )(shapes[0], sketch_signs[0], merge_sketch)
    total_coords = coords * n
    basis = basis.reshape(coords, width) * math.sqrt(total_coords)
    scores = scores * (4.0 * math.sqrt(width / total_coords))
    return basis[None], scores[None]


def solution(mesh):
    placed = (P("cohort", None, "coord"), P("cohort", None, None), P())
    return jax.shard_map(
        on_device,
        mesh=mesh,
        in_specs=placed,
        out_specs=(P("cohort", "coord", None), P("cohort", "coord", None)),
        check_vma=False,
    )
```

time: 113 us -> 86.1 us (0.76)
  matrix products: 10.5 us -> 0 us
  Pallas kernels: 89.3 us -> 80.4 us
  local copies, waits for them, and re-layouts: 5.82 us -> 1.98 us
  waiting for transfers between devices: 2.61 us -> 0 us
  starting transfers between devices: 2.54 us -> 0 us
  other arithmetic: 0 us -> 2.14 us
    dot_general x5 -> x0, matrix products: 10.5 us -> none  [the longest x2 4.39 us: mix(): jnp.matmul(own, own_map, precision=HIGHEST)]
    pallas_call x8 -> x1, Pallas kernels: 89.3 us -> 80.4 us  [on_device(): pl.pallas_call(functools.partial(whole_kernel, n, tile), out_shape=(jax.S...]
    ppermute x4 -> x0, waiting for transfers between devices: 2.61 us -> none  [swap(): lax.ppermute(value, 'cohort', [(i, i ^ distance) for i in range(size)])]
    unnamed x6 -> x4, local copies, waits for them, and re-layouts: 4.53 us -> 1.98 us
    ppermute x4 -> x0, starting transfers between devices: 2.54 us -> none  [swap(): lax.ppermute(value, 'cohort', [(i, i ^ distance) for i in range(size)])]
    mul x0 -> x1, other arithmetic: none -> 1.5 us  [on_device(): basis = basis.reshape(coords, width) * math.sqrt(total_coords)]
    squeeze x2 -> x0, local copies, waits for them, and re-layouts: 1.28 us -> none  [the longest x1 0.64 us: on_device(): merge_sketch[0][side]]
  transfers between devices with their start and end apart: 4 -> 0, of which waited for: 1 -> 0; matrix products, arithmetic and copies ran while one was open for 5% -> 0% of each run, Pallas kernels for 38% -> 0%
where the time goes in v1:
time: 86.1 us; the launch traced here: 85.2 us
  Pallas kernels  80.4 us (93%)
  other arithmetic  2.14 us (2%)
  local copies, waits for them, and re-layouts  1.98 us (2%)
    pallas_call x1, Pallas kernels, on_device(): pl.pallas_call(functools.partial(whole_kernel, n, tile), out_shape=(jax.S...  80.4 us
    unnamed x4, local copies, waits for them, and re-layouts  1.98 us

profile of v1, /device:TPU:0, one launch (start us, length us, event | category | flops | bytes accessed | tf_op | source)
XLA Modules:
  0.0 85.2 jit_solution(11613698659491887175)
XLA Ops:
  0.6 0.0 copy-start
  0.6 1.0 %copy-done = s32[1,1024,128]{2,1,0:T(8,128)S(1)} copy-done((s32[1,1024,128]{2,1,0:T(8,128)S(1)}, s32[1,1024,128]{2,1,0:T(8,128)}, u32[]{:S(2)}) %copy-start) | copy-done | bytes 524312
  1.7 0.0 copy-start.1
  1.7 0.9 %copy-done.1 = f32[2,2,128,128]{3,2,1,0:T(8,128)S(1)} copy-done((f32[2,2,128,128]{3,2,1,0:T(8,128)S(1)}, f32[2,2,128,128]{3,2,1,0:T(8,128)}, u32[]{:S(2)}) %copy-start.1) | copy-done | bytes 262168
  2.6 80.4 %shape_pca.1 = (f32[2,2048,128]{2,1,0:T(8,128)S(1)}, f32[128,128]{1,0:T(8,128)S(1)}) custom-call(bf16[1024,4096]{1,0:T(8,128)(2,1)} %bitcast.6, s32[1024,128]{1,0:T(8,128)S(1)} %bitcast.5, f32[2,2,128,128]{3,2,1,0:T(8,128)S(1)} %copy-done.1), custom_call_target="tpu_custom_call" | custom-call | tf_op jit(solution)/shard_map/shape_pca/pallas_call | solution.py:405
  83.1 1.5 %broadcast_multiply_fusion = f32[2,2048,128]{2,1,0:T(8,128)} fusion(f32[2,2048,128]{2,1,0:T(8,128)S(1)} %get-tuple-element.4), kind=kLoop, calls=%fused_computation | loop fusion | flops 524288 | bytes 4194304 | tf_op jit(solution)/shard_map/mul | solution.py:456
  84.6 0.6 multiply_bitcast_fusion
Async XLA Ops:
  0.6 1.0 %copy-start = (s32[1,1024,128]{2,1,0:T(8,128)S(1)}, s32[1,1024,128]{2,1,0:T(8,128)}, u32[]{:S(2)}) copy-start(s32[1,1024,128]{2,1,0:T(8,128)} %param.4) | copy-start | bytes 1572868
  1.7 0.9 %copy-start.1 = (f32[2,2,128,128]{3,2,1,0:T(8,128)S(1)}, f32[2,2,128,128]{3,2,1,0:T(8,128)}, u32[]{:S(2)}) copy-start(f32[2,2,128,128]{3,2,1,0:T(8,128)} %merge_ref.1) | copy-start | bytes 786436

commit v2 on v1

--- a/solution.py
+++ b/solution.py
@@ -160,12 +160,12 @@
 
 def whole_kernel(
     n, tile, shapes_ref, signs_ref, merge_ref, basis_ref, scores_ref,
-    held, signs, merge, turned, given, pairs, mixed, stacked, maps, outer, x_ref, narrow,
-    wide, products, gram_part, gram_recv, gram, low_part, low_recv, low_gram,
+    held, signs, merge, turned, given, pairs, far, mixed, stacks, low_maps, up_maps, outer, x_ref,
+    wide, products, projected, gram_part, gram_recv, gram, low_part, low_recv, low_gram,
     up_part, up_recv, up_gram, up_other, score_part, score_recv,
-    loaded, small, give_send, give_got, gram_send, gram_got, gram_send2, gram_got2,
-    low_send, low_got, low_send2, low_got2, up_send, up_got, up_send2, up_got2,
-    cross_send, cross_got, basis_send, basis_got, score_send, score_got, map_send, map_got,
+    loaded, small, give_send, give_got, far_send, far_got, core_send, core_got,
+    cross_send, cross_got, gram_send, gram_got, gram_send2, gram_got2, score_send, score_got,
+    low_send, low_got, low_send2, low_got2, up_send, up_got, up_send2, up_got2, map_send, map_got,
 ):
     coord = lax.axis_index("coord")
     cohort = lax.axis_index("cohort")
@@ -174,16 +174,20 @@
     base = cohort - side
     partner = {"cohort": cohort + 1 - 2 * side}
     across = {"cohort": cohort + 2 - 4 * upper}
+    corner = {"cohort": cohort + 2 - 4 * upper + 1 - 2 * side}
     line = (coord, n, lambda r: {"coord": r})
     pair = (
         coord * 2 + side, 2 * n, lambda r: {"coord": r // 2, "cohort": base + lax.rem(r, 2)}
     )
     chunks = held.shape[0] // 2
-    half = chunks * tile
+    early = chunks // 2
     width = turned.shape[0]
 
     def rows_of(c):
         return pl.ds(pl.multiple_of(c * tile, tile), tile)
+
+    def turn_of(which, i):
+        return lax.rem(i + which * early, chunks)
 
     small_copies = [
         pltpu.make_async_copy(signs_ref, signs, small.at[0]),
@@ -197,9 +201,9 @@
             shapes_ref.at[:, pl.ds(at, tile)], held.at[h * chunks + c], loaded.at[h, c]
         )
 
-    for h in (1 - side, side):
-        for c in range(chunks):
-            load(h, c).start()
+    for i in range(chunks):
+        load(1 - side, turn_of(upper, i)).start()
+        load(side, turn_of(upper, i)).start()
 
     barrier = pltpu.get_barrier_semaphore()
     me, size, ident = pair
@@ -208,19 +212,28 @@
             barrier, inc=1, device_id=ident(lax.rem(me + d, size)), device_id_type=MESH
         )
     pl.semaphore_signal(barrier, inc=1, device_id=across, device_id_type=MESH)
-    for copy in small_copies:
-        copy.wait()
+    pl.semaphore_signal(barrier, inc=1, device_id=corner, device_id_type=MESH)
+    wide[...] = jnp.zeros_like(wide)
+    products[...] = jnp.zeros_like(products)
+    small_copies[0].wait()
     turned[...] = signs[...].astype(F32).T.astype(BF16)
-    for l in range(2):
-        outer[l] = dot_high(merge[l, 0], merge[l, 0], ((0,), (0,))) + dot_high(
-            merge[l, 1], merge[l, 1], ((0,), (0,))
-        )
-    wide[...] = jnp.zeros_like(wide)
-    pl.semaphore_wait(barrier, size)
+    pl.semaphore_wait(barrier, size + 1)
 
     def give(c):
         return remote(
             given.at[rows_of(c)], pairs.at[side, rows_of(c)], give_send.at[c], give_got.at[c], partner
+        )
+
+    def far_given(i):
+        return remote(
+            given.at[rows_of(turn_of(upper, i))], far.at[side, i],
+            far_send.at[0, i], far_got.at[0, i], corner,
+        )
+
+    def far_mine(i):
+        return remote(
+            pairs.at[side, rows_of(turn_of(upper, i))], far.at[side, i],
+            far_send.at[1, i], far_got.at[1, i], across,
         )
 
     def sketch(h, c):
@@ -234,24 +247,29 @@
         wide[...] += dot(flat.astype(BF16), jnp.concatenate([high, mid], axis=1))
         return rows
 
-    def first(c, carry):
+    def first(i, carry):
+        c = turn_of(upper, i)
+        given[rows_of(c)] = sketch(1 - side, c)
+        far_given(i).start()
+        give(c).start()
+        pairs[side, rows_of(c)] = sketch(side, c)
+        far_mine(i).start()
+        return carry
+
+    def second(i, carry):
+        c = turn_of(upper, i)
         given[rows_of(c)] = sketch(1 - side, c)
         give(c).start()
-        return carry
-
-    def second(c, carry):
         pairs[side, rows_of(c)] = sketch(side, c)
         return carry
 
-    lax.fori_loop(0, chunks, first, 0)
-    lax.fori_loop(0, chunks, second, 0)
+    lax.fori_loop(0, early, first, 0)
+    lax.fori_loop(early, chunks, second, 0)
     turn = wide[:, width:]
     own = wide[:, :width] + turn + turn.T
     gram_part[...] = own.reshape(gram_part.shape)
     copies = scatter(gram_part, gram_recv, line, gram_send, gram_got)
     start(copies)
-
-    products[...] = jnp.zeros_like(products)
 
     def cross(c, carry):
         give(c).wait_recv()
@@ -265,130 +283,166 @@
     start(gathered)
     low_copies = scatter(low_part, low_recv, pair, low_send, low_got)
     start(low_copies)
+    small_copies[1].wait()
+    for l in range(2):
+        outer[l] = dot_high(merge[l, 0], merge[l, 0], ((0,), (0,))) + dot_high(
+            merge[l, 1], merge[l, 1], ((0,), (0,))
+        )
     received(gathered)
 
     inverse_of(gram[...].reshape(width, width), x_ref)
-    maps[0, side] = dot_high(x_ref[...], merge[0, side], ((0,), (0,)))
-    map_swap = remote(maps.at[0, side], maps.at[0, side], map_send.at[0], map_got.at[0], partner)
-    map_swap.start()
+    low_maps[upper, side] = dot_high(x_ref[...], merge[0, side], ((0,), (0,)))
+    own_map = low_maps.at[upper, side]
+    map_copies = [
+        remote(own_map, own_map, map_send.at[i], map_got.at[i], device)
+        for i, device in enumerate((partner, across, corner))
+    ]
+    start(map_copies)
     low_gram[pair[0]] = summed(low_part, low_recv, pair, low_copies)
     low_gathered = spread(low_gram, pair, low_send2, low_got2)
     start(low_gathered)
-    map_swap.wait_recv()
+    map_copies[0].wait_recv()
     for i in range(2):
-        stack_map(stacked, i, maps[0, i])
+        stack_map(stacks.at[0], i, low_maps[upper, i])
 
     def ship(c):
-        return remote(
-            mixed.at[upper, rows_of(c)], mixed.at[upper, rows_of(c)],
-            cross_send.at[c], cross_got.at[c], across,
-        )
-
-    def turn_of(which, i):
-        return lax.rem(i + which * (chunks // 2), chunks)
-
-    def blend(i, carry):
+        rows = mixed.at[upper, side, rows_of(c)]
+        return remote(rows, rows, cross_send.at[c], cross_got.at[c], across)
+
+    def share(which, c):
+        far_side = lax.rem(which + upper, 2)
+        rows = mixed.at[far_side, side, rows_of(c)]
+        return remote(rows, rows, core_send.at[which, c], core_got.at[which, c], partner)
+
+    def blend(i):
         c = turn_of(upper, i)
-        mixed[upper, rows_of(c)] = mix_rows(pairs[0, rows_of(c)], pairs[1, rows_of(c)], stacked)
-        ship(c).start()
-        return carry
-
-    lax.fori_loop(0, chunks, blend, 0)
-    received(low_gathered)
-    inner = dot_high(
-        maps[0, 0],
-        dot_high(low_gram[...].reshape(width, width), maps[0, 1], ((1,), (0,))),
-        ((0,), (0,)),
-    )
-    inverse_of(outer[0] + inner + inner.T, x_ref)
-    maps[1, upper] = dot_high(x_ref[...], merge[1, upper], ((0,), (0,)))
-    across_swap = remote(maps.at[1, upper], maps.at[1, upper], map_send.at[1], map_got.at[1], across)
-    across_swap.start()
+        mixed[upper, side, rows_of(c)] = mix_rows(
+            pairs[0, rows_of(c)], pairs[1, rows_of(c)], stacks.at[0]
+        )
+        share(0, c).start()
+        return c
+
+    for i in range(early, chunks):
+        c = blend(i)
+        if i < chunks - 1:
+            ship(c).start()
+    late = turn_of(upper, chunks - 1)
+    for i in range(early):
+        blend(i)
+    received(map_copies[1:])
+    for i in range(2):
+        stack_map(stacks.at[1], i, low_maps[1 - upper, i])
 
     products[...] = jnp.zeros_like(products)
 
     def meet(i, carry):
         c = turn_of(1 - upper, i)
-        ship(c).wait_recv()
-        products[...] += cross_product(mixed[0, rows_of(c)], mixed[1, rows_of(c)])
-        return carry
-
-    lax.fori_loop(0, chunks // 2, meet, 0)
+        far_given(i).wait_recv()
+        far_mine(i).wait_recv()
+        mixed[1 - upper, side, rows_of(c)] = mix_rows(far[0, i], far[1, i], stacks.at[1])
+        share(1, c).start()
+        products[...] += cross_product(mixed[0, side, rows_of(c)], mixed[1, side, rows_of(c)])
+        return carry
+
+    lax.fori_loop(0, early, meet, 0)
     up_part[...] = products[...].reshape(up_part.shape)
     up_copies = scatter(up_part, up_recv, pair, up_send, up_got)
     start(up_copies)
+    received(low_gathered)
+    inner = dot_high(
+        low_maps[upper, 0],
+        dot_high(low_gram[...].reshape(width, width), low_maps[upper, 1], ((1,), (0,))),
+        ((0,), (0,)),
+    )
+    inverse_of(outer[0] + inner + inner.T, x_ref)
+    up_maps[upper] = dot_high(x_ref[...], merge[1, upper], ((0,), (0,)))
     up_other[upper] = summed(up_part, up_recv, pair, up_copies)
-    up_swap = remote(up_other.at[upper], up_other.at[upper], map_send.at[2], map_got.at[2], across)
+    up_swap = remote(up_other.at[upper], up_other.at[upper], map_send.at[3], map_got.at[3], across)
     up_swap.start()
+    across_swap = remote(
+        up_maps.at[upper], up_maps.at[upper], map_send.at[4], map_got.at[4], across
+    )
+    across_swap.start()
+    ship(late).start()
+
+    projected[...] = jnp.zeros_like(projected)
+
+    def project(h, c):
+        rows = jnp.concatenate(
+            [mixed[0, h, rows_of(c)].astype(BF16), mixed[1, h, rows_of(c)].astype(BF16)], axis=1
+        )
+        projected[...] += dot(held[h * chunks + c], rows)
+
+    def project_early(i, carry):
+        c = turn_of(1 - upper, i)
+        project(side, c)
+        share(0, c).wait_recv()
+        share(1, c).wait_recv()
+        project(1 - side, c)
+        return carry
+
+    def project_late(i, carry):
+        c = turn_of(1 - upper, i)
+        ship(c).wait_recv()
+        share(1, c).start()
+        project(side, c)
+        return carry
+
+    def project_last(i, carry):
+        c = turn_of(1 - upper, i)
+        share(0, c).wait_recv()
+        share(1, c).wait_recv()
+        project(1 - side, c)
+        return carry
+
+    lax.fori_loop(0, 1, project_early, 0)
     up_swap.wait_recv()
     up_gram[pair[0]] = up_other[0] + up_other[1]
     up_gathered = spread(up_gram, pair, up_send2, up_got2)
     start(up_gathered)
+    lax.fori_loop(1, early, project_early, 0)
+    lax.fori_loop(early, chunks, project_late, 0)
     across_swap.wait_recv()
     received(up_gathered)
     inner = dot_high(
-        maps[1, 0],
-        dot_high(up_gram[...].reshape(width, width), maps[1, 1], ((1,), (0,))),
+        up_maps[0],
+        dot_high(up_gram[...].reshape(width, width), up_maps[1], ((1,), (0,))),
         ((0,), (0,)),
     )
     inverse_of(outer[1] + inner + inner.T, x_ref)
     for i in range(2):
-        stack_map(stacked, i, dot_high(maps[1, i], x_ref[...], ((1,), (1,))))
-
-    def hand(c):
-        return remote(
-            basis_ref.at[side, rows_of(c)], basis_ref.at[side, rows_of(c)],
-            basis_send.at[c], basis_got.at[c], partner,
-        )
-
-    def finish(c):
-        rows = mix_rows(mixed[0, rows_of(c)], mixed[1, rows_of(c)], stacked)
-        basis_ref[side, rows_of(c)] = rows
-        narrow[side * chunks + c] = rows.astype(BF16)
-        hand(c).start()
-
-
-    def arriving(i, carry):
-        c = turn_of(1 - upper, i)
-        ship(c).wait_recv()
-        finish(c)
-        return carry
-
-    def local(i, carry):
-        finish(turn_of(1 - upper, i))
-        return carry
-
-    lax.fori_loop(0, chunks // 2, local, 0)
-    lax.fori_loop(chunks // 2, chunks, arriving, 0)
+        stack_map(stacks.at[0], i, dot_high(up_maps[i], x_ref[...], ((1,), (1,))))
+    lax.fori_loop(early, chunks, project_last, 0)
 
     block = score_part.shape[1]
-    order = [lax.rem(coord + d, n) for d in list(range(1, n)) + [0]]
-
-    def taken(peer, h):
-        rows = pl.ds(pl.multiple_of(peer * block, block), block)
-        total = dot(held[h * chunks, rows], narrow[h * chunks])
-        for c in range(1, chunks):
-            total = total + dot(held[h * chunks + c, rows], narrow[h * chunks + c])
-        return total
-
-    for peer in order:
-        score_part[peer] = taken(peer, side)
-    for c in range(chunks):
-        hand(c).wait_recv()
-        narrow[(1 - side) * chunks + c] = basis_ref[1 - side, rows_of(c)].astype(BF16)
     score_copies = scatter(score_part, score_recv, line, score_send, score_got)
-    for d, peer in zip(list(range(1, n)) + [0], order):
-        score_part[peer] = score_part[peer] + taken(peer, 1 - side)
+    for d in list(range(1, n)) + [0]:
+        peer = lax.rem(coord + d, n)
+        rows = projected[pl.ds(pl.multiple_of(peer * block, block), block), :]
+        score_part[peer] = mix_rows(rows[:, :width], rows[:, width:], stacks.at[0])
         if d:
             score_copies[d - 1].start()
+
+    def finish(c, carry):
+        for h in range(2):
+            basis_ref[h, rows_of(c)] = mix_rows(
+                mixed[0, h, rows_of(c)], mixed[1, h, rows_of(c)], stacks.at[0]
+            )
+        return carry
+
+    lax.fori_loop(0, chunks, finish, 0)
     scores_ref[...] = summed(score_part, score_recv, line, score_copies)
 
     sent(copies + gathered + low_copies + low_gathered + up_copies + up_gathered + score_copies)
-    sent([map_swap, across_swap, up_swap])
+    sent(map_copies + [across_swap, up_swap])
+    for i in range(early):
+        far_given(i).wait_send()
+        far_mine(i).wait_send()
+        ship(turn_of(upper, early + i)).wait_send()
     for c in range(chunks):
         give(c).wait_send()
-        ship(c).wait_send()
-        hand(c).wait_send()
+        share(0, c).wait_send()
+        share(1, c).wait_send()
 
 
 def on_device(shapes, sketch_signs, merge_sketch):
@@ -408,7 +462,7 @@
             jax.ShapeDtypeStruct((2, half, width), F32),
             jax.ShapeDtypeStruct((rows, width), F32),
         ),
-        in_specs=[pl.BlockSpec(memory_space=pl.ANY)] * 3,
+        in_specs=[pl.BlockSpec(memory_space=pltpu.HBM)] * 3,
         out_specs=(pl.BlockSpec(memory_space=vmem), pl.BlockSpec(memory_space=vmem)),
         scratch_shapes=[
             vmem((2 * chunks, subjects, tile), BF16),
@@ -417,41 +471,42 @@
             vmem((width, subjects), BF16),
             vmem((half, width), F32),
             vmem((2, half, width), F32),
-            vmem((2, half, width), F32),
-            vmem((6 * width, width), BF16),
+            vmem((2, chunks // 2, tile, width), F32),
+            vmem((2, 2, half, width), F32),
+            vmem((2, 6 * width, width), BF16),
             vmem((2, 2, width, width), F32),
             vmem((2, width, width), F32),
+            vmem((2, width, width), F32),
             vmem((width, width), F32),
-            vmem((2 * chunks, tile, width), BF16),
             vmem((width, 2 * width), F32),
             vmem((width, width), F32),
-            vmem(line, F32),
-            vmem(line, F32),
-            vmem(line, F32),
-            vmem(pair, F32),
-            vmem(pair, F32),
-            vmem(pair, F32),
-            vmem(pair, F32),
-            vmem(pair, F32),
-            vmem(pair, F32),
+            vmem((subjects, 2 * width), F32),
+        ]
+        + [vmem(line, F32)] * 3
+        + [vmem(pair, F32)] * 6
+        + [
             vmem((2,) + pair[1:], F32),
             vmem((n, rows, width), F32),
             vmem((n, rows, width), F32),
             dma((2, chunks)),
             dma((2,)),
-            dma((chunks,)),
-            dma((chunks,)),
         ]
-        + [dma((n,))] * 4
+        + [dma((chunks,))] * 2
+        + [dma((2, chunks // 2))] * 2
+        + [dma((2, chunks))] * 2
+        + [dma((chunks,))] * 2
+        + [dma((n,))] * 6
         + [dma((2 * n,))] * 8
-        + [dma((chunks,))] * 4
-        + [dma((n,))] * 2
-        + [dma((3,))] * 2,
+        + [dma((5,))] * 2,
         compiler_params=pltpu.CompilerParams(
             collective_id=0, has_side_effects=True, vmem_limit_bytes=48 * 1024 * 1024
         ),
         name="shape_pca",
-    )(shapes[0], sketch_signs[0], merge_sketch)
+    )(
+        shapes[0],
+        pltpu.with_memory_space_constraint(sketch_signs[0], pltpu.HBM),
+        pltpu.with_memory_space_constraint(merge_sketch, pltpu.HBM),
+    )
     total_coords = coords * n
     basis = basis.reshape(coords, width) * math.sqrt(total_coords)
     scores = scores * (4.0 * math.sqrt(width / total_coords))

time: 86.1 us -> 75.7 us (0.88)
  Pallas kernels: 80.4 us -> 71.6 us
  local copies, waits for them, and re-layouts: 1.98 us -> 0 us
    pallas_call x1, Pallas kernels: 80.4 us -> 71.6 us  [on_device(): pl.pallas_call(functools.partial(whole_kernel, n, tile), out_shape=(jax.S...]
    unnamed x4 -> x0, local copies, waits for them, and re-layouts: 1.98 us -> none
where the time goes in v2:
time: 75.7 us; the launch traced here: 74.4 us
  Pallas kernels  71.6 us (95%)
  other arithmetic  2.14 us (3%)
    pallas_call x1, Pallas kernels, on_device(): pl.pallas_call(functools.partial(whole_kernel, n, tile), out_shape=(jax.S...  71.6 us

profile of v2, /device:TPU:0, one launch (start us, length us, event | category | flops | bytes accessed | tf_op | source)
XLA Modules:
  0.0 74.4 jit_solution(8495126791260949398)
XLA Ops:
  0.6 71.6 %shape_pca.1 = (f32[2,2048,128]{2,1,0:T(8,128)S(1)}, f32[128,128]{1,0:T(8,128)S(1)}) custom-call(bf16[1024,4096]{1,0:T(8,128)(2,1)} %bitcast.5, s32[1024,128]{1,0:T(8,128)} %bitcast.7, f32[2,2,128,128]{3,2,1,0:T(8,128)} %merge_ref.1), custom_call_target="tpu_custom_call" | custom-call | tf_op jit(solution)/shard_map/shape_pca/pallas_call | solution.py:459
  72.2 1.5 %broadcast_multiply_fusion = f32[2,2048,128]{2,1,0:T(8,128)} fusion(f32[2,2048,128]{2,1,0:T(8,128)S(1)} %get-tuple-element.4), kind=kLoop, calls=%fused_computation | loop fusion | flops 524288 | bytes 4194304 | tf_op jit(solution)/shard_map/mul | solution.py:511
  73.7 0.6 multiply_bitcast_fusion

commit v3 on v2

--- a/solution.py
+++ b/solution.py
@@ -73,15 +73,14 @@
             terms = [terms[i] + terms[i + 1] for i in range(0, len(terms), 2)]
         return terms[0]
 
-    left = gram.reshape(tiles, step, size)
-    right = jnp.stack([(lane == sub + t * step).astype(F32) for t in range(tiles)])
+    both = [gram[t * step : (t + 1) * step, :] for t in range(tiles)]
     for t in range(tiles):
         at = t * step
-        head, head_x = left[0], right[0]
-        cols = [full(head[:, at + k : at + k + 1]) for k in range(step)]
+        inside = (lane >= at) & (lane < at + step)
+        cols = [full(both[t][:, at + k : at + k + 1]) for k in range(step)]
         e = [[full(cols[k][i : i + 1, :]) for k in range(i + 1)] for i in range(step)]
+        head = jnp.where(inside, (lane - at == sub).astype(F32), both[t])
         rows = [full(head[i : i + 1, :]) for i in range(step)]
-        rows_x = [full(head_x[i : i + 1, :]) for i in range(step)]
         f = {}
         inv = []
         for s in range(step):
@@ -92,23 +91,17 @@
                     e[i][k] = e[i][k] - f[i, s] * e[k][s]
             for i in range(s + 1, step):
                 rows[i] = rows[i] - f[i, s] * rows[s]
-                rows_x[i] = rows_x[i] - f[i, s] * rows_x[s]
-        out = rows_x[0] * lax.rsqrt(e[0][0])
+        out = rows[0] * lax.rsqrt(e[0][0])
         for s in range(1, step):
-            out = jnp.where(sub == s, rows_x[s] * lax.rsqrt(e[s][s]), out)
-        x_ref[at : at + step, :] = out
-        if t + 1 == tiles:
-            break
+            out = jnp.where(sub == s, rows[s] * lax.rsqrt(e[s][s]), out)
+        x_ref[at : at + step, :] = jnp.where(lane < at + step, out, 0.0)
         rows = [rows[s] * inv[s] for s in range(step)]
-        rows_x = [rows_x[s] * inv[s] for s in range(step)]
-        for s in range(step - 2, -1, -1):
-            for i in range(s + 1, step):
-                rows[s] = rows[s] - f[i, s] * rows[i]
-                rows_x[s] = rows_x[s] - f[i, s] * rows_x[i]
-        left, right = left[1:], right[1:]
-        c = [jnp.broadcast_to(left[:, :, at + s : at + s + 1], left.shape) for s in range(step)]
-        left = left - total([c[s] * rows[s][None] for s in range(step)])
-        right = right - total([c[s] * rows_x[s][None] for s in range(step)])
+        for u in range(t + 1, tiles):
+            c = [full(both[u][:, at + s : at + s + 1]) for s in range(step)]
+            for s in range(step):
+                for r in range(s):
+                    c[s] = c[s] - f[s, r] * c[r]
+            both[u] = jnp.where(inside, 0.0, both[u]) - total([c[s] * rows[s] for s in range(step)])
 
 
 def remote(src, dst, send, got, device):
@@ -159,9 +152,9 @@
 
 
 def whole_kernel(
-    n, tile, shapes_ref, signs_ref, merge_ref, basis_ref, scores_ref,
+    n, tile, scale, grow, shapes_ref, signs_ref, merge_ref, basis_ref, scores_ref,
     held, signs, merge, turned, given, pairs, far, mixed, stacks, low_maps, up_maps, outer, x_ref,
-    wide, products, projected, gram_part, gram_recv, gram, low_part, low_recv, low_gram,
+    flats, parts, wide, products, projected, gram_part, gram_recv, gram, low_part, low_recv, low_gram,
     up_part, up_recv, up_gram, up_other, score_part, score_recv,
     loaded, small, give_send, give_got, far_send, far_got, core_send, core_got,
     cross_send, cross_got, gram_send, gram_got, gram_send2, gram_got2, score_send, score_got,
@@ -195,15 +188,13 @@
     ]
     start(small_copies)
 
-    def load(h, c):
-        at = pl.multiple_of((h * chunks + c) * tile, tile)
-        return pltpu.make_async_copy(
-            shapes_ref.at[:, pl.ds(at, tile)], held.at[h * chunks + c], loaded.at[h, c]
-        )
-
-    for i in range(chunks):
-        load(1 - side, turn_of(upper, i)).start()
-        load(side, turn_of(upper, i)).start()
+    def load(j):
+        h = side if j % 2 else 1 - side
+        at = pl.multiple_of((h * chunks + turn_of(upper, j // 2)) * tile, tile)
+        return pltpu.make_async_copy(shapes_ref.at[:, pl.ds(at, tile)], held.at[j], loaded.at[j])
+
+    for j in range(2 * chunks):
+        load(j).start()
 
     barrier = pltpu.get_barrier_semaphore()
     me, size, ident = pair
@@ -215,9 +206,6 @@
     pl.semaphore_signal(barrier, inc=1, device_id=corner, device_id_type=MESH)
     wide[...] = jnp.zeros_like(wide)
     products[...] = jnp.zeros_like(products)
-    small_copies[0].wait()
-    turned[...] = signs[...].astype(F32).T.astype(BF16)
-    pl.semaphore_wait(barrier, size + 1)
 
     def give(c):
         return remote(
@@ -236,42 +224,52 @@
             far_send.at[1, i], far_got.at[1, i], across,
         )
 
-    def sketch(h, c):
-        load(h, c).wait()
-        block = held.at[h * chunks + c]
+    def center(j):
+        load(j).wait()
+        block = held.at[j]
         mean = jnp.sum(block[...].astype(F32), axis=0, keepdims=True) * (1.0 / block.shape[0])
         block[...] = (block[...].astype(F32) - mean).astype(BF16)
-        flat = dot(turned[...], block[...])
+
+    def sketch(j):
+        flat = dot(turned[...], held[j])
         rows = flat.T
+        if j % 2:
+            pairs[side, rows_of(turn_of(upper, j // 2))] = rows
+        else:
+            given[rows_of(turn_of(upper, j // 2))] = rows
         high, mid = split(rows)
-        wide[...] += dot(flat.astype(BF16), jnp.concatenate([high, mid], axis=1))
-        return rows
-
-    def first(i, carry):
-        c = turn_of(upper, i)
-        given[rows_of(c)] = sketch(1 - side, c)
-        far_given(i).start()
-        give(c).start()
-        pairs[side, rows_of(c)] = sketch(side, c)
-        far_mine(i).start()
-        return carry
-
-    def second(i, carry):
-        c = turn_of(upper, i)
-        given[rows_of(c)] = sketch(1 - side, c)
-        give(c).start()
-        pairs[side, rows_of(c)] = sketch(side, c)
-        return carry
-
-    lax.fori_loop(0, early, first, 0)
-    lax.fori_loop(early, chunks, second, 0)
+        flats[j % 2] = flat.astype(BF16)
+        parts[j % 2, :, :width] = high
+        parts[j % 2, :, width:] = mid
+
+    def send_sketch(j):
+        i = j // 2
+        if i < early:
+            (far_mine(i) if j % 2 else far_given(i)).start()
+        if j % 2 == 0:
+            give(turn_of(upper, i)).start()
+
+    center(0)
+    small_copies[0].wait()
+    turned[...] = signs[...].astype(F32).T.astype(BF16)
+    for j in range(2 * chunks):
+        if j + 1 < 2 * chunks:
+            center(j + 1)
+        sketch(j)
+        if j:
+            wide[...] += dot(flats[(j - 1) % 2], parts[(j - 1) % 2])
+        else:
+            pl.semaphore_wait(barrier, size + 1)
+        send_sketch(j)
+    wide[...] += dot(flats[1], parts[1])
     turn = wide[:, width:]
     own = wide[:, :width] + turn + turn.T
     gram_part[...] = own.reshape(gram_part.shape)
     copies = scatter(gram_part, gram_recv, line, gram_send, gram_got)
     start(copies)
 
-    def cross(c, carry):
+    def cross(i, carry):
+        c = turn_of(upper, i)
         give(c).wait_recv()
         products[...] += cross_product(pairs[0, rows_of(c)], pairs[1, rows_of(c)])
         return carry
@@ -323,10 +321,7 @@
         return c
 
     for i in range(early, chunks):
-        c = blend(i)
-        if i < chunks - 1:
-            ship(c).start()
-    late = turn_of(upper, chunks - 1)
+        ship(blend(i)).start()
     for i in range(early):
         blend(i)
     received(map_copies[1:])
@@ -363,36 +358,37 @@
         up_maps.at[upper], up_maps.at[upper], map_send.at[4], map_got.at[4], across
     )
     across_swap.start()
-    ship(late).start()
 
     projected[...] = jnp.zeros_like(projected)
 
-    def project(h, c):
+    def project(h, i):
+        c = turn_of(1 - upper, i)
         rows = jnp.concatenate(
             [mixed[0, h, rows_of(c)].astype(BF16), mixed[1, h, rows_of(c)].astype(BF16)], axis=1
         )
-        projected[...] += dot(held[h * chunks + c], rows)
-
-    def project_early(i, carry):
+        place = 2 * lax.rem(i + early, chunks) + lax.rem(h + side + 1, 2)
+        projected[...] += dot(held[place], rows)
+
+    def project_given(i):
         c = turn_of(1 - upper, i)
-        project(side, c)
         share(0, c).wait_recv()
         share(1, c).wait_recv()
-        project(1 - side, c)
+        project(1 - side, i)
+
+    def project_early(i, carry):
+        project(side, i)
+        project_given(i)
         return carry
 
     def project_late(i, carry):
         c = turn_of(1 - upper, i)
         ship(c).wait_recv()
         share(1, c).start()
-        project(side, c)
+        project(side, i)
         return carry
 
     def project_last(i, carry):
-        c = turn_of(1 - upper, i)
-        share(0, c).wait_recv()
-        share(1, c).wait_recv()
-        project(1 - side, c)
+        project_given(i)
         return carry
 
     lax.fori_loop(0, 1, project_early, 0)
@@ -411,7 +407,9 @@
     )
     inverse_of(outer[1] + inner + inner.T, x_ref)
     for i in range(2):
-        stack_map(stacks.at[0], i, dot_high(up_maps[i], x_ref[...], ((1,), (1,))))
+        last = dot_high(up_maps[i], x_ref[...], ((1,), (1,)))
+        stack_map(stacks.at[0], i, last * scale)
+        stack_map(stacks.at[1], i, last * grow)
     lax.fori_loop(early, chunks, project_last, 0)
 
     block = score_part.shape[1]
@@ -426,7 +424,7 @@
     def finish(c, carry):
         for h in range(2):
             basis_ref[h, rows_of(c)] = mix_rows(
-                mixed[0, h, rows_of(c)], mixed[1, h, rows_of(c)], stacks.at[0]
+                mixed[0, h, rows_of(c)], mixed[1, h, rows_of(c)], stacks.at[1]
             )
         return carry
 
@@ -445,6 +443,16 @@
         share(1, c).wait_send()
 
 
+def store_kernel(basis_ref, scores_ref, basis_out, scores_out, sems):
+    copies = [
+        pltpu.make_async_copy(basis_ref.at[h], basis_out.at[h], sems.at[h]) for h in range(2)
+    ]
+    copies.append(pltpu.make_async_copy(scores_ref, scores_out, sems.at[2]))
+    start(copies)
+    for copy in copies:
+        copy.wait()
+
+
 def on_device(shapes, sketch_signs, merge_sketch):
     n = lax.axis_size("coord")
     _, subjects, coords = shapes.shape
@@ -455,9 +463,11 @@
     rows = subjects // n
     line = (n, width // n, width)
     pair = (2 * n, width // (2 * n), width)
+    scale = 4.0 * math.sqrt(width / (coords * n))
+    grow = math.sqrt(coords * n)
     vmem, dma = pltpu.VMEM, pltpu.SemaphoreType.DMA
     basis, scores = pl.pallas_call(
-        functools.partial(whole_kernel, n, tile),
+        functools.partial(whole_kernel, n, tile, scale, grow),
         out_shape=(
             jax.ShapeDtypeStruct((2, half, width), F32),
             jax.ShapeDtypeStruct((rows, width), F32),
@@ -478,6 +488,8 @@
             vmem((2, width, width), F32),
             vmem((2, width, width), F32),
             vmem((width, width), F32),
+            vmem((2, width, tile), BF16),
+            vmem((2, tile, 2 * width), BF16),
             vmem((width, 2 * width), F32),
             vmem((width, width), F32),
             vmem((subjects, 2 * width), F32),
@@ -488,7 +500,7 @@
             vmem((2,) + pair[1:], F32),
             vmem((n, rows, width), F32),
             vmem((n, rows, width), F32),
-            dma((2, chunks)),
+            dma((2 * chunks,)),
             dma((2,)),
         ]
         + [dma((chunks,))] * 2
@@ -507,10 +519,21 @@
         pltpu.with_memory_space_constraint(sketch_signs[0], pltpu.HBM),
         pltpu.with_memory_space_constraint(merge_sketch, pltpu.HBM),
     )
-    total_coords = coords * n
-    basis = basis.reshape(coords, width) * math.sqrt(total_coords)
-    scores = scores * (4.0 * math.sqrt(width / total_coords))
-    return basis[None], scores[None]
+    basis, scores = pl.pallas_call(
+        store_kernel,
+        out_shape=(
+            jax.ShapeDtypeStruct(basis.shape, F32),
+            jax.ShapeDtypeStruct(scores.shape, F32),
+        ),
+        in_specs=[pl.BlockSpec(memory_space=vmem)] * 2,
+        out_specs=(pl.BlockSpec(memory_space=pltpu.HBM),) * 2,
+        scratch_shapes=[dma((3,))],
+        name="store",
+    )(
+        pltpu.with_memory_space_constraint(basis, pltpu.VMEM),
+        pltpu.with_memory_space_constraint(scores, pltpu.VMEM),
+    )
+    return basis.reshape(1, coords, width), scores[None]
 
 
 def solution(mesh):

time: 75.7 us -> 72.8 us (0.962)
  other arithmetic: 2.14 us -> 0 us
  Pallas kernels: 71.6 us -> 70.7 us
    mul x1 -> x0, other arithmetic: 1.5 us -> none  [on_device(): basis = basis.reshape(coords, width) * math.sqrt(total_coords)]
    pallas_call x1 -> x2, Pallas kernels: 71.6 us -> 70.7 us  [the longest x1 69.4 us: on_device(): pl.pallas_call(functools.partial(whole_kernel, n, tile, scale, grow), out...]
where the time goes in v3:
time: 72.8 us; the launch traced here: 71.5 us
  Pallas kernels  70.7 us (97%)
  between operations  0.82 us (1%)
    pallas_call x1, Pallas kernels, on_device(): pl.pallas_call(functools.partial(whole_kernel, n, tile, scale, grow), out...  69.4 us

profile of v3, /device:TPU:0, one launch (start us, length us, event | category | flops | bytes accessed | tf_op | source)
XLA Modules:
  0.0 71.5 jit_solution(10314517716727590563)
XLA Ops:
  0.6 69.4 %shape_pca.1 = (f32[2,2048,128]{2,1,0:T(8,128)S(1)}, f32[128,128]{1,0:T(8,128)S(1)}) custom-call(bf16[1024,4096]{1,0:T(8,128)(2,1)} %bitcast.4, s32[1024,128]{1,0:T(8,128)} %bitcast.5, f32[2,2,128,128]{3,2,1,0:T(8,128)} %merge_ref.1), custom_call_target="tpu_custom_call" | custom-call | tf_op jit(solution)/shard_map/shape_pca/pallas_call | solution.py:469
  70.0 1.3 %store.1 = (f32[2,2048,128]{2,1,0:T(8,128)}, f32[128,128]{1,0:T(8,128)}) custom-call(f32[2,2048,128]{2,1,0:T(8,128)S(1)} %get-tuple-element.6.basis_ref, f32[128,128]{1,0:T(8,128)S(1)} %get-tuple-element.7.scores_ref), custom_call_target="tpu_custom_call" | custom-call | tf_op jit(solution)/shard_map/store/pallas_call | solution.py:522

commit v4 on v3

--- a/solution.py
+++ b/solution.py
@@ -174,10 +174,16 @@
     )
     chunks = held.shape[0] // 2
     early = chunks // 2
+    piece = tile // 2
+    raw = far.shape[1]
     width = turned.shape[0]
 
     def rows_of(c):
         return pl.ds(pl.multiple_of(c * tile, tile), tile)
+
+    def piece_of(which, p):
+        at = turn_of(which, p // 2) * tile + (p % 2) * piece
+        return pl.ds(pl.multiple_of(at, piece), piece)
 
     def turn_of(which, i):
         return lax.rem(i + which * early, chunks)
@@ -193,7 +199,7 @@
         at = pl.multiple_of((h * chunks + turn_of(upper, j // 2)) * tile, tile)
         return pltpu.make_async_copy(shapes_ref.at[:, pl.ds(at, tile)], held.at[j], loaded.at[j])
 
-    for j in range(2 * chunks):
+    for j in range(3):
         load(j).start()
 
     barrier = pltpu.get_barrier_semaphore()
@@ -212,20 +218,21 @@
             given.at[rows_of(c)], pairs.at[side, rows_of(c)], give_send.at[c], give_got.at[c], partner
         )
 
-    def far_given(i):
+    def far_given(p):
         return remote(
-            given.at[rows_of(turn_of(upper, i))], far.at[side, i],
-            far_send.at[0, i], far_got.at[0, i], corner,
-        )
-
-    def far_mine(i):
+            given.at[piece_of(upper, p)], far.at[side, p], far_send.at[0, p], far_got.at[0, p], corner
+        )
+
+    def far_mine(p):
         return remote(
-            pairs.at[side, rows_of(turn_of(upper, i))], far.at[side, i],
-            far_send.at[1, i], far_got.at[1, i], across,
+            pairs.at[side, piece_of(upper, p)], far.at[side, p],
+            far_send.at[1, p], far_got.at[1, p], across,
         )
 
     def center(j):
         load(j).wait()
+        if j + 3 < 2 * chunks:
+            load(j + 3).start()
         block = held.at[j]
         mean = jnp.sum(block[...].astype(F32), axis=0, keepdims=True) * (1.0 / block.shape[0])
         block[...] = (block[...].astype(F32) - mean).astype(BF16)
@@ -244,8 +251,8 @@
 
     def send_sketch(j):
         i = j // 2
-        if i < early:
-            (far_mine(i) if j % 2 else far_given(i)).start()
+        for p in range(2 * i, min(2 * i + 2, raw)):
+            (far_mine(p) if j % 2 else far_given(p)).start()
         if j % 2 == 0:
             give(turn_of(upper, i)).start()
 
@@ -303,9 +310,9 @@
     for i in range(2):
         stack_map(stacks.at[0], i, low_maps[upper, i])
 
-    def ship(c):
-        rows = mixed.at[upper, side, rows_of(c)]
-        return remote(rows, rows, cross_send.at[c], cross_got.at[c], across)
+    def ship(which, p):
+        rows = mixed.at[which, side, piece_of(which, p)]
+        return remote(rows, rows, cross_send.at[p], cross_got.at[p], across)
 
     def share(which, c):
         far_side = lax.rem(which + upper, 2)
@@ -320,26 +327,28 @@
         share(0, c).start()
         return c
 
-    for i in range(early, chunks):
-        ship(blend(i)).start()
-    for i in range(early):
+    for i in list(range(raw // 2, chunks)) + list(range(raw // 2)):
         blend(i)
+        for p in range(max(2 * i, raw), 2 * i + 2):
+            ship(upper, p).start()
     received(map_copies[1:])
     for i in range(2):
         stack_map(stacks.at[1], i, low_maps[1 - upper, i])
 
     products[...] = jnp.zeros_like(products)
 
-    def meet(i, carry):
-        c = turn_of(1 - upper, i)
-        far_given(i).wait_recv()
-        far_mine(i).wait_recv()
-        mixed[1 - upper, side, rows_of(c)] = mix_rows(far[0, i], far[1, i], stacks.at[1])
-        share(1, c).start()
-        products[...] += cross_product(mixed[0, side, rows_of(c)], mixed[1, side, rows_of(c)])
-        return carry
-
-    lax.fori_loop(0, early, meet, 0)
+    for p in range(2 * early):
+        c = turn_of(1 - upper, p // 2)
+        rows = piece_of(1 - upper, p)
+        if p < raw:
+            far_given(p).wait_recv()
+            far_mine(p).wait_recv()
+            mixed[1 - upper, side, rows] = mix_rows(far[0, p], far[1, p], stacks.at[1])
+        else:
+            ship(1 - upper, p).wait_recv()
+        if p % 2:
+            share(1, c).start()
+        products[...] += cross_product(mixed[0, side, rows], mixed[1, side, rows])
     up_part[...] = products[...].reshape(up_part.shape)
     up_copies = scatter(up_part, up_recv, pair, up_send, up_got)
     start(up_copies)
@@ -380,37 +389,22 @@
         project_given(i)
         return carry
 
-    def project_late(i, carry):
-        c = turn_of(1 - upper, i)
-        ship(c).wait_recv()
-        share(1, c).start()
-        project(side, i)
-        return carry
-
-    def project_last(i, carry):
-        project_given(i)
-        return carry
-
     lax.fori_loop(0, 1, project_early, 0)
     up_swap.wait_recv()
     up_gram[pair[0]] = up_other[0] + up_other[1]
     up_gathered = spread(up_gram, pair, up_send2, up_got2)
     start(up_gathered)
     lax.fori_loop(1, early, project_early, 0)
-    lax.fori_loop(early, chunks, project_late, 0)
+    for i in range(early, chunks):
+        for p in range(2 * i, 2 * i + 2):
+            ship(1 - upper, p).wait_recv()
+        share(1, turn_of(1 - upper, i)).start()
+        project(side, i)
     across_swap.wait_recv()
-    received(up_gathered)
-    inner = dot_high(
-        up_maps[0],
-        dot_high(up_gram[...].reshape(width, width), up_maps[1], ((1,), (0,))),
-        ((0,), (0,)),
-    )
-    inverse_of(outer[1] + inner + inner.T, x_ref)
     for i in range(2):
-        last = dot_high(up_maps[i], x_ref[...], ((1,), (1,)))
-        stack_map(stacks.at[0], i, last * scale)
-        stack_map(stacks.at[1], i, last * grow)
-    lax.fori_loop(early, chunks, project_last, 0)
+        stack_map(stacks.at[0], i, up_maps[i])
+    for i in range(early, chunks):
+        project_given(i)
 
     block = score_part.shape[1]
     score_copies = scatter(score_part, score_recv, line, score_send, score_got)
@@ -421,6 +415,16 @@
         if d:
             score_copies[d - 1].start()
 
+    received(up_gathered)
+    inner = dot_high(
+        up_maps[0],
+        dot_high(up_gram[...].reshape(width, width), up_maps[1], ((1,), (0,))),
+        ((0,), (0,)),
+    )
+    inverse_of(outer[1] + inner + inner.T, x_ref)
+    for i in range(2):
+        stack_map(stacks.at[1], i, dot_high(up_maps[i], x_ref[...], ((1,), (1,))) * grow)
+
     def finish(c, carry):
         for h in range(2):
             basis_ref[h, rows_of(c)] = mix_rows(
@@ -429,14 +433,17 @@
         return carry
 
     lax.fori_loop(0, chunks, finish, 0)
-    scores_ref[...] = summed(score_part, score_recv, line, score_copies)
+    total = summed(score_part, score_recv, line, score_copies)
+    scores_ref[...] = dot_high(total, x_ref[...], ((1,), (1,))) * scale
 
     sent(copies + gathered + low_copies + low_gathered + up_copies + up_gathered + score_copies)
     sent(map_copies + [across_swap, up_swap])
-    for i in range(early):
-        far_given(i).wait_send()
-        far_mine(i).wait_send()
-        ship(turn_of(upper, early + i)).wait_send()
+    for p in range(2 * chunks):
+        if p < raw:
+            far_given(p).wait_send()
+            far_mine(p).wait_send()
+        else:
+            ship(upper, p).wait_send()
     for c in range(chunks):
         give(c).wait_send()
         share(0, c).wait_send()
@@ -460,6 +467,7 @@
     half = coords // 2
     tile = math.gcd(half // 2, 512)
     chunks = half // tile
+    raw = 3 * chunks // 4
     rows = subjects // n
     line = (n, width // n, width)
     pair = (2 * n, width // (2 * n), width)
@@ -481,7 +489,7 @@
             vmem((width, subjects), BF16),
             vmem((half, width), F32),
             vmem((2, half, width), F32),
-            vmem((2, chunks // 2, tile, width), F32),
+            vmem((2, raw, tile // 2, width), F32),
             vmem((2, 2, half, width), F32),
             vmem((2, 6 * width, width), BF16),
             vmem((2, 2, width, width), F32),
@@ -504,9 +512,9 @@
             dma((2,)),
         ]
         + [dma((chunks,))] * 2
-        + [dma((2, chunks // 2))] * 2
+        + [dma((2, raw))] * 2
         + [dma((2, chunks))] * 2
-        + [dma((chunks,))] * 2
+        + [dma((2 * chunks,))] * 2
         + [dma((n,))] * 6
         + [dma((2 * n,))] * 8
         + [dma((5,))] * 2,

time: 72.8 us -> 63.2 us (0.87)
  the two profiles are of different devices: /device:TPU:0 before, /device:TPU:13 now
where the time goes in v4:
time: 63.2 us; the launch traced here: 63.1 us
  Pallas kernels  62.3 us (99%)
  between operations  0.82 us (1%)
    pallas_call x1, Pallas kernels, on_device(): pl.pallas_call(functools.partial(whole_kernel, n, tile, scale, grow), out...  60.9 us
    pallas_call x1, Pallas kernels, on_device(): pl.pallas_call(store_kernel, out_shape=(jax.ShapeDtypeStruct(basis.shape,...  1.35 us

profile of v4, /device:TPU:13, one launch (start us, length us, event | category | flops | bytes accessed | tf_op | source)
XLA Modules:
  0.0 63.1 jit_solution(8696274411914876611)
XLA Ops:
  0.6 60.9 %shape_pca.1 = (f32[2,2048,128]{2,1,0:T(8,128)S(1)}, f32[128,128]{1,0:T(8,128)S(1)}) custom-call(bf16[1024,4096]{1,0:T(8,128)(2,1)} %bitcast.4, s32[1024,128]{1,0:T(8,128)} %bitcast.5, f32[2,2,128,128]{3,2,1,0:T(8,128)} %merge_ref.1), custom_call_target="tpu_custom_call" | custom-call | tf_op jit(solution)/shard_map/shape_pca/pallas_call | solution.py:477
  61.6 1.3 %store.1 = (f32[2,2048,128]{2,1,0:T(8,128)}, f32[128,128]{1,0:T(8,128)}) custom-call(f32[2,2048,128]{2,1,0:T(8,128)S(1)} %get-tuple-element.6.basis_ref, f32[128,128]{1,0:T(8,128)S(1)} %get-tuple-element.7.scores_ref), custom_call_target="tpu_custom_call" | custom-call | tf_op jit(solution)/shard_map/store/pallas_call | solution.py:530

commit v5 on v4

--- a/solution.py
+++ b/solution.py
@@ -58,7 +58,7 @@
     return dot(rows, stacked[...])
 
 
-def inverse_of(gram, x_ref):
+def inverse_of(gram, x_ref, between=None):
     size = gram.shape[1]
     step = 8
     tiles = size // step
@@ -102,6 +102,8 @@
                 for r in range(s):
                     c[s] = c[s] - f[s, r] * c[r]
             both[u] = jnp.where(inside, 0.0, both[u]) - total([c[s] * rows[s] for s in range(step)])
+        if between is not None:
+            between(t, tiles)
 
 
 def remote(src, dst, send, got, device):
@@ -155,9 +157,10 @@
     n, tile, scale, grow, shapes_ref, signs_ref, merge_ref, basis_ref, scores_ref,
     held, signs, merge, turned, given, pairs, far, mixed, stacks, low_maps, up_maps, outer, x_ref,
     flats, parts, wide, products, projected, gram_part, gram_recv, gram, low_part, low_recv, low_gram,
-    up_part, up_recv, up_gram, up_other, score_part, score_recv,
+    up_part, up_recv, up_gram, up_other, score_part, hop_recv, score_recv,
     loaded, small, give_send, give_got, far_send, far_got, core_send, core_got,
-    cross_send, cross_got, gram_send, gram_got, gram_send2, gram_got2, score_send, score_got,
+    cross_send, cross_got, gram_send, gram_got, gram_send2, gram_got2,
+    hop_send, hop_got, score_send, score_got,
     low_send, low_got, low_send2, low_got2, up_send, up_got, up_send2, up_got2, map_send, map_got,
 ):
     coord = lax.axis_index("coord")
@@ -389,16 +392,16 @@
         project_given(i)
         return carry
 
-    lax.fori_loop(0, 1, project_early, 0)
-    up_swap.wait_recv()
-    up_gram[pair[0]] = up_other[0] + up_other[1]
+    lax.fori_loop(0, early, project_early, 0)
     up_gathered = spread(up_gram, pair, up_send2, up_got2)
-    start(up_gathered)
-    lax.fori_loop(1, early, project_early, 0)
     for i in range(early, chunks):
         for p in range(2 * i, 2 * i + 2):
             ship(1 - upper, p).wait_recv()
         share(1, turn_of(1 - upper, i)).start()
+        if i == chunks - 1:
+            up_swap.wait_recv()
+            up_gram[pair[0]] = up_other[0] + up_other[1]
+            start(up_gathered)
         project(side, i)
     across_swap.wait_recv()
     for i in range(2):
@@ -407,13 +410,42 @@
         project_given(i)
 
     block = score_part.shape[1]
-    score_copies = scatter(score_part, score_recv, line, score_send, score_got)
-    for d in list(range(1, n)) + [0]:
-        peer = lax.rem(coord + d, n)
-        rows = projected[pl.ds(pl.multiple_of(peer * block, block), block), :]
-        score_part[peer] = mix_rows(rows[:, :width], rows[:, width:], stacks.at[0])
-        if d:
-            score_copies[d - 1].start()
+    groups = n // 2
+    group = coord // 2
+    bit = lax.rem(coord, 2)
+
+    def score_block(place):
+        rows = projected[pl.ds(pl.multiple_of(place * block, block), block), :]
+        score_part[place] = mix_rows(rows[:, :width], rows[:, width:], stacks.at[0])
+
+    def hop(d):
+        place = 2 * lax.rem(group + d, groups) + 1 - bit
+        return remote(
+            score_part.at[place], hop_recv.at[d], hop_send.at[d], hop_got.at[d],
+            {"coord": coord + 1 - 2 * bit},
+        )
+
+    def relay(d):
+        place = 2 * lax.rem(group + d, groups) + bit
+        return remote(
+            score_part.at[place], score_recv.at[d], score_send.at[d], score_got.at[d],
+            {"coord": place},
+        )
+
+    order = list(range(1, groups)) + [0]
+    for d in order:
+        score_block(2 * lax.rem(group + d, groups) + 1 - bit)
+        hop(d).start()
+    for d in order:
+        score_block(2 * lax.rem(group + d, groups) + bit)
+
+    def between(t, tiles):
+        for d in range(1, groups):
+            if t == (tiles - 4) * d // (groups - 1):
+                hop(d).wait_recv()
+                place = 2 * lax.rem(group + d, groups) + bit
+                score_part[place] = score_part[place] + hop_recv[d]
+                relay(d).start()
 
     received(up_gathered)
     inner = dot_high(
@@ -421,7 +453,7 @@
         dot_high(up_gram[...].reshape(width, width), up_maps[1], ((1,), (0,))),
         ((0,), (0,)),
     )
-    inverse_of(outer[1] + inner + inner.T, x_ref)
+    inverse_of(outer[1] + inner + inner.T, x_ref, between)
     for i in range(2):
         stack_map(stacks.at[1], i, dot_high(up_maps[i], x_ref[...], ((1,), (1,))) * grow)
 
@@ -433,11 +465,19 @@
         return carry
 
     lax.fori_loop(0, chunks, finish, 0)
-    total = summed(score_part, score_recv, line, score_copies)
+    hop(0).wait_recv()
+    total = score_part[coord] + hop_recv[0]
+    for d in range(1, groups):
+        relay(d).wait_recv()
+        total = total + score_recv[d]
     scores_ref[...] = dot_high(total, x_ref[...], ((1,), (1,))) * scale
 
-    sent(copies + gathered + low_copies + low_gathered + up_copies + up_gathered + score_copies)
+    sent(copies + gathered + low_copies + low_gathered + up_copies + up_gathered)
     sent(map_copies + [across_swap, up_swap])
+    for d in range(groups):
+        hop(d).wait_send()
+        if d:
+            relay(d).wait_send()
     for p in range(2 * chunks):
         if p < raw:
             far_given(p).wait_send()
@@ -467,7 +507,7 @@
     half = coords // 2
     tile = math.gcd(half // 2, 512)
     chunks = half // tile
-    raw = 3 * chunks // 4
+    raw = chunks
     rows = subjects // n
     line = (n, width // n, width)
     pair = (2 * n, width // (2 * n), width)
@@ -507,7 +547,8 @@
         + [
             vmem((2,) + pair[1:], F32),
             vmem((n, rows, width), F32),
-            vmem((n, rows, width), F32),
+            vmem((n // 2, rows, width), F32),
+            vmem((n // 2, rows, width), F32),
             dma((2 * chunks,)),
             dma((2,)),
         ]
@@ -515,7 +556,8 @@
         + [dma((2, raw))] * 2
         + [dma((2, chunks))] * 2
         + [dma((2 * chunks,))] * 2
-        + [dma((n,))] * 6
+        + [dma((n,))] * 4
+        + [dma((n // 2,))] * 4
         + [dma((2 * n,))] * 8
         + [dma((5,))] * 2,
         compiler_params=pltpu.CompilerParams(

time: 63.2 us -> 64.2 us (1.016)
  the two profiles are of different devices: /device:TPU:13 before, /device:TPU:0 now
where the time goes in v5:
time: 64.2 us; the launch traced here: 64 us
  Pallas kernels  63.2 us (98%)
  between operations  0.82 us (1%)
    pallas_call x1, Pallas kernels, on_device(): pl.pallas_call(functools.partial(whole_kernel, n, tile, scale, grow), out...  61.9 us
    pallas_call x1, Pallas kernels, on_device(): pl.pallas_call(store_kernel, out_shape=(jax.ShapeDtypeStruct(basis.shape,...  1.35 us

profile of v5, /device:TPU:0, one launch (start us, length us, event | category | flops | bytes accessed | tf_op | source)
XLA Modules:
  0.0 64.0 jit_solution(10338292957432801152)
XLA Ops:
  0.6 61.9 %shape_pca.1 = (f32[2,2048,128]{2,1,0:T(8,128)S(1)}, f32[128,128]{1,0:T(8,128)S(1)}) custom-call(bf16[1024,4096]{1,0:T(8,128)(2,1)} %bitcast.4, s32[1024,128]{1,0:T(8,128)} %bitcast.5, f32[2,2,128,128]{3,2,1,0:T(8,128)} %merge_ref.1), custom_call_target="tpu_custom_call" | custom-call | tf_op jit(solution)/shard_map/shape_pca/pallas_call | solution.py:517
  62.5 1.3 %store.1 = (f32[2,2048,128]{2,1,0:T(8,128)}, f32[128,128]{1,0:T(8,128)}) custom-call(f32[2,2048,128]{2,1,0:T(8,128)S(1)} %get-tuple-element.6.basis_ref, f32[128,128]{1,0:T(8,128)S(1)} %get-tuple-element.7.scores_ref), custom_call_target="tpu_custom_call" | custom-call | tf_op jit(solution)/shard_map/store/pallas_call | solution.py:572

commit v6 on v5

--- a/solution.py
+++ b/solution.py
@@ -157,7 +157,7 @@
     n, tile, scale, grow, shapes_ref, signs_ref, merge_ref, basis_ref, scores_ref,
     held, signs, merge, turned, given, pairs, far, mixed, stacks, low_maps, up_maps, outer, x_ref,
     flats, parts, wide, products, projected, gram_part, gram_recv, gram, low_part, low_recv, low_gram,
-    up_part, up_recv, up_gram, up_other, score_part, hop_recv, score_recv,
+    up_part, up_recv, up_gram, up_sides, score_part, hop_recv, score_recv,
     loaded, small, give_send, give_got, far_send, far_got, core_send, core_got,
     cross_send, cross_got, gram_send, gram_got, gram_send2, gram_got2,
     hop_send, hop_got, score_send, score_got,
@@ -363,9 +363,9 @@
     )
     inverse_of(outer[0] + inner + inner.T, x_ref)
     up_maps[upper] = dot_high(x_ref[...], merge[1, upper], ((0,), (0,)))
-    up_other[upper] = summed(up_part, up_recv, pair, up_copies)
-    up_swap = remote(up_other.at[upper], up_other.at[upper], map_send.at[3], map_got.at[3], across)
-    up_swap.start()
+    up_gram[pair[0]] = summed(up_part, up_recv, pair, up_copies)
+    up_gathered = spread(up_gram, pair, up_send2, up_got2)
+    start(up_gathered)
     across_swap = remote(
         up_maps.at[upper], up_maps.at[upper], map_send.at[4], map_got.at[4], across
     )
@@ -393,15 +393,14 @@
         return carry
 
     lax.fori_loop(0, early, project_early, 0)
-    up_gathered = spread(up_gram, pair, up_send2, up_got2)
+    received(up_gathered)
+    up_sides[upper] = up_gram[...].reshape(width, width)
+    up_swap = remote(up_sides.at[upper], up_sides.at[upper], map_send.at[3], map_got.at[3], across)
+    up_swap.start()
     for i in range(early, chunks):
         for p in range(2 * i, 2 * i + 2):
             ship(1 - upper, p).wait_recv()
         share(1, turn_of(1 - upper, i)).start()
-        if i == chunks - 1:
-            up_swap.wait_recv()
-            up_gram[pair[0]] = up_other[0] + up_other[1]
-            start(up_gathered)
         project(side, i)
     across_swap.wait_recv()
     for i in range(2):
@@ -447,10 +446,10 @@
                 score_part[place] = score_part[place] + hop_recv[d]
                 relay(d).start()
 
-    received(up_gathered)
+    up_swap.wait_recv()
     inner = dot_high(
         up_maps[0],
-        dot_high(up_gram[...].reshape(width, width), up_maps[1], ((1,), (0,))),
+        dot_high(up_sides[0] + up_sides[1], up_maps[1], ((1,), (0,))),
         ((0,), (0,)),
     )
     inverse_of(outer[1] + inner + inner.T, x_ref, between)
@@ -507,7 +506,7 @@
     half = coords // 2
     tile = math.gcd(half // 2, 512)
     chunks = half // tile
-    raw = chunks
+    raw = max(1, 3 * chunks // 4)
     rows = subjects // n
     line = (n, width // n, width)
     pair = (2 * n, width // (2 * n), width)
@@ -545,7 +544,7 @@
         + [vmem(line, F32)] * 3
         + [vmem(pair, F32)] * 6
         + [
-            vmem((2,) + pair[1:], F32),
+            vmem((2, width, width), F32),
             vmem((n, rows, width), F32),
             vmem((n // 2, rows, width), F32),
             vmem((n // 2, rows, width), F32),

time: 64.2 us -> 60.8 us (0.947)
  Pallas kernels: 63.2 us -> 59.8 us
    pallas_call x1, Pallas kernels: 61.9 us -> 58.5 us  [on_device(): pl.pallas_call(functools.partial(whole_kernel, n, tile, scale, grow), out...]
where the time goes in v6:
time: 60.8 us; the launch traced here: 60.7 us
  Pallas kernels  59.8 us (98%)
  between operations  0.82 us (1%)
    pallas_call x1, Pallas kernels, on_device(): pl.pallas_call(functools.partial(whole_kernel, n, tile, scale, grow), out...  58.5 us
    pallas_call x1, Pallas kernels, on_device(): pl.pallas_call(store_kernel, out_shape=(jax.ShapeDtypeStruct(basis.shape,...  1.35 us

profile of v6, /device:TPU:0, one launch (start us, length us, event | category | flops | bytes accessed | tf_op | source)
XLA Modules:
  0.0 60.7 jit_solution(9496972099402068645)
XLA Ops:
  0.6 58.5 %shape_pca.1 = (f32[2,2048,128]{2,1,0:T(8,128)S(1)}, f32[128,128]{1,0:T(8,128)S(1)}) custom-call(bf16[1024,4096]{1,0:T(8,128)(2,1)} %bitcast.4, s32[1024,128]{1,0:T(8,128)} %bitcast.5, f32[2,2,128,128]{3,2,1,0:T(8,128)} %merge_ref.1), custom_call_target="tpu_custom_call" | custom-call | tf_op jit(solution)/shard_map/shape_pca/pallas_call | solution.py:516
  59.1 1.3 %store.1 = (f32[2,2048,128]{2,1,0:T(8,128)}, f32[128,128]{1,0:T(8,128)}) custom-call(f32[2,2048,128]{2,1,0:T(8,128)S(1)} %get-tuple-element.6.basis_ref, f32[128,128]{1,0:T(8,128)S(1)} %get-tuple-element.7.scores_ref), custom_call_target="tpu_custom_call" | custom-call | tf_op jit(solution)/shard_map/store/pallas_call | solution.py:571

commit v7 on v6

--- a/solution.py
+++ b/solution.py
@@ -303,7 +303,7 @@
     own_map = low_maps.at[upper, side]
     map_copies = [
         remote(own_map, own_map, map_send.at[i], map_got.at[i], device)
-        for i, device in enumerate((partner, across, corner))
+        for i, device in enumerate((partner, across))
     ]
     start(map_copies)
     low_gram[pair[0]] = summed(low_part, low_recv, pair, low_copies)
@@ -334,7 +334,11 @@
         blend(i)
         for p in range(max(2 * i, raw), 2 * i + 2):
             ship(upper, p).start()
-    received(map_copies[1:])
+    map_copies[1].wait_recv()
+    far_map = low_maps.at[1 - upper, side]
+    map_copies.append(remote(far_map, far_map, map_send.at[2], map_got.at[2], partner))
+    map_copies[2].start()
+    map_copies[2].wait_recv()
     for i in range(2):
         stack_map(stacks.at[1], i, low_maps[1 - upper, i])
 
@@ -413,9 +417,11 @@
     group = coord // 2
     bit = lax.rem(coord, 2)
 
-    def score_block(place):
-        rows = projected[pl.ds(pl.multiple_of(place * block, block), block), :]
-        score_part[place] = mix_rows(rows[:, :width], rows[:, width:], stacks.at[0])
+    def score_pair(g):
+        rows = projected[pl.ds(pl.multiple_of(2 * g * block, 2 * block), 2 * block), :]
+        both = mix_rows(rows[:, :width], rows[:, width:], stacks.at[0])
+        score_part[2 * g] = both[:block]
+        score_part[2 * g + 1] = both[block:]
 
     def hop(d):
         place = 2 * lax.rem(group + d, groups) + 1 - bit
@@ -431,12 +437,9 @@
             {"coord": place},
         )
 
-    order = list(range(1, groups)) + [0]
-    for d in order:
-        score_block(2 * lax.rem(group + d, groups) + 1 - bit)
+    for d in list(range(1, groups)) + [0]:
+        score_pair(lax.rem(group + d, groups))
         hop(d).start()
-    for d in order:
-        score_block(2 * lax.rem(group + d, groups) + bit)
 
     def between(t, tiles):
         for d in range(1, groups):

time: 60.8 us -> 60 us (0.987)
  Pallas kernels: 59.8 us -> 59 us
    pallas_call x1, Pallas kernels: 58.5 us -> 57.7 us  [on_device(): pl.pallas_call(functools.partial(whole_kernel, n, tile, scale, grow), out...]
where the time goes in v7:
time: 60 us; the launch traced here: 59.9 us
  Pallas kernels  59 us (98%)
  between operations  0.82 us (1%)
    pallas_call x1, Pallas kernels, on_device(): pl.pallas_call(functools.partial(whole_kernel, n, tile, scale, grow), out...  57.7 us
    pallas_call x1, Pallas kernels, on_device(): pl.pallas_call(store_kernel, out_shape=(jax.ShapeDtypeStruct(basis.shape,...  1.35 us

profile of v7, /device:TPU:0, one launch (start us, length us, event | category | flops | bytes accessed | tf_op | source)
XLA Modules:
  0.0 59.9 jit_solution(1350767656585601433)
XLA Ops:
  0.6 57.7 %shape_pca.1 = (f32[2,2048,128]{2,1,0:T(8,128)S(1)}, f32[128,128]{1,0:T(8,128)S(1)}) custom-call(bf16[1024,4096]{1,0:T(8,128)(2,1)} %bitcast.4, s32[1024,128]{1,0:T(8,128)} %bitcast.5, f32[2,2,128,128]{3,2,1,0:T(8,128)} %merge_ref.1), custom_call_target="tpu_custom_call" | custom-call | tf_op jit(solution)/shard_map/shape_pca/pallas_call | solution.py:519
  58.3 1.3 %store.1 = (f32[2,2048,128]{2,1,0:T(8,128)}, f32[128,128]{1,0:T(8,128)}) custom-call(f32[2,2048,128]{2,1,0:T(8,128)S(1)} %get-tuple-element.6.basis_ref, f32[128,128]{1,0:T(8,128)S(1)} %get-tuple-element.7.scores_ref), custom_call_target="tpu_custom_call" | custom-call | tf_op jit(solution)/shard_map/store/pallas_call | solution.py:574

commit v8 on v7

--- a/solution.py
+++ b/solution.py
@@ -195,7 +195,7 @@
         pltpu.make_async_copy(signs_ref, signs, small.at[0]),
         pltpu.make_async_copy(merge_ref, merge, small.at[1]),
     ]
-    start(small_copies)
+    small_copies[0].start()
 
     def load(j):
         h = side if j % 2 else 1 - side
@@ -204,6 +204,7 @@
 
     for j in range(3):
         load(j).start()
+    small_copies[1].start()
 
     barrier = pltpu.get_barrier_semaphore()
     me, size, ident = pair
@@ -459,14 +460,11 @@
     for i in range(2):
         stack_map(stacks.at[1], i, dot_high(up_maps[i], x_ref[...], ((1,), (1,))) * grow)
 
-    def finish(c, carry):
+    for c in range(chunks):
         for h in range(2):
             basis_ref[h, rows_of(c)] = mix_rows(
                 mixed[0, h, rows_of(c)], mixed[1, h, rows_of(c)], stacks.at[1]
             )
-        return carry
-
-    lax.fori_loop(0, chunks, finish, 0)
     hop(0).wait_recv()
     total = score_part[coord] + hop_recv[0]
     for d in range(1, groups):

time: 60 us -> 60.1 us (level)
  no operation moved by 1% of the time
where the time goes in v8:
time: 60.1 us; the launch traced here: 59.9 us
  Pallas kernels  59.1 us (98%)
  between operations  0.82 us (1%)
    pallas_call x1, Pallas kernels, on_device(): pl.pallas_call(functools.partial(whole_kernel, n, tile, scale, grow), out...  57.8 us
    pallas_call x1, Pallas kernels, on_device(): pl.pallas_call(store_kernel, out_shape=(jax.ShapeDtypeStruct(basis.shape,...  1.35 us

profile of v8, /device:TPU:0, one launch (start us, length us, event | category | flops | bytes accessed | tf_op | source)
XLA Modules:
  0.0 59.9 jit_solution(9039054478150851000)
XLA Ops:
  0.6 57.8 %shape_pca.1 = (f32[2,2048,128]{2,1,0:T(8,128)S(1)}, f32[128,128]{1,0:T(8,128)S(1)}) custom-call(bf16[1024,4096]{1,0:T(8,128)(2,1)} %bitcast.4, s32[1024,128]{1,0:T(8,128)} %bitcast.5, f32[2,2,128,128]{3,2,1,0:T(8,128)} %merge_ref.1), custom_call_target="tpu_custom_call" | custom-call | tf_op jit(solution)/shard_map/shape_pca/pallas_call | solution.py:517
  58.4 1.3 %store.1 = (f32[2,2048,128]{2,1,0:T(8,128)}, f32[128,128]{1,0:T(8,128)}) custom-call(f32[2,2048,128]{2,1,0:T(8,128)S(1)} %get-tuple-element.6.basis_ref, f32[128,128]{1,0:T(8,128)S(1)} %get-tuple-element.7.scores_ref), custom_call_target="tpu_custom_call" | custom-call | tf_op jit(solution)/shard_map/store/pallas_call | solution.py:572
